TPU v7x, 512 devices: a whole 4x4x16 slice. The times are simulated.
512 devices in a mesh: row: 32 (over x_hi, z), col: 16 (over y, x_lo, core).
Axes of the slice: x: 4 (x_hi: 2, x_lo: 2; x = x_hi * 2 + x_lo), y: 4, z: 16, core: 2. Of those that a mesh axis runs over, the one named last changes fastest.
Arguments:
- left: bfloat16 [128, 16384], P('col', 'row'), may hold values from -6 to 6
- right: bfloat16 [128, 16384], P('row', 'col'), may hold values from -6 to 6
- pair_in: bfloat16 [512, 512, 128], P('row', 'col'), may hold values from -6 to 6
- pair_cot: bfloat16 [512, 512, 128], P('row', 'col'), may hold values from -6 to 6
- ln_gain: float32 [128], replicated, may hold values from 0.25 to 1.75
- out_weight: bfloat16 [1024, 128], replicated, may hold values from -2 to 2
- out_bias: float32 [128], replicated, may hold values from -3 to 3
- trans_up: bfloat16 [128, 512], replicated, may hold values from -0.5 to 0.5
- trans_down: bfloat16 [512, 128], replicated, may hold values from -0.25 to 0.25
Outputs:
- pair_out: bfloat16 [512, 512, 128], P('row', 'col')
- grad_left: bfloat16 [128, 16384], P('col', 'row')
- grad_right: bfloat16 [128, 16384], P('row', 'col')
All inputs are finite; a program needn't handle non-finite values.
Results may differ from a plain program's by a relative error of at most 0.01.
The roundings to bfloat16 on the way count: a program that leaves them out, or rounds other values in their place, can miss the bound.
Values may be sent and summed in bfloat16 or wider, within the bound.
No kernel may reach another device: no remote copies, remote signals or barrier semaphores. Data moves between devices by JAX's collectives and lax.ppermute only.
A program may use at most 64 MiB of HBM per device.

v0:
```python
import jax
import jax.numpy as jnp
from jax import lax
from jax.sharding import PartitionSpec as P

C = 32
SEQS = 128


def laid_out(tiles, dim):
    dims = list(tiles.shape[1:])
    dims[dim] *= tiles.shape[0]
    return jnp.moveaxis(tiles, 0, dim).reshape(dims)


def sent_to_all(shard, axis):
    copies = jnp.broadcast_to(shard, (lax.axis_size(axis), *shard.shape))
    return lax.all_to_all(copies, axis, split_axis=0, concat_axis=0, tiled=True)


def collect(shard, axis, dim):
    return laid_out(sent_to_all(shard, axis), dim)


def cut_along(shard, dim, length):
    before, after = (shard.shape[:dim], shard.shape[dim + 1 :])
    return jnp.moveaxis(shard.reshape(*before, length, -1, *after), dim, 0)


def sum_at_owner(shard, axis, dim):
    tiles = cut_along(shard, dim, lax.axis_size(axis))
    arrived = lax.all_to_all(tiles, axis, split_axis=0, concat_axis=0, tiled=True)
    return arrived.astype(jnp.float32).sum(axis=0)


def pair_block(outer, pair_in, pair_cot, ln_gain, out_weight, out_bias, trans_up, trans_down):
    update = jnp.einsum("ijk,kd->ijd", outer, out_weight, preferred_element_type=jnp.float32)
    middle = pair_in.astype(jnp.float32) + update + out_bias
    centre = jnp.mean(middle, axis=-1, keepdims=True)
    centred = middle - centre
    spread = jnp.mean(centred * centred, axis=-1, keepdims=True)
    inverse = lax.rsqrt(spread + 1e-05)
    normal_x = centred * inverse
    normed = (normal_x * ln_gain).astype(jnp.bfloat16)
    preact = jnp.einsum("ijk,kf->ijf", normed, trans_up, preferred_element_type=jnp.float32)
    hidden = jnp.maximum(preact, 0.0).astype(jnp.bfloat16)
    down = jnp.einsum("ijf,fk->ijk", hidden, trans_down, preferred_element_type=jnp.float32)
    pair_out = (middle + down).astype(jnp.bfloat16)
    back = jnp.einsum("ijk,fk->ijf", pair_cot, trans_down, preferred_element_type=jnp.float32)
    d_hidden = jnp.where(preact > 0.0, back, 0.0).astype(jnp.bfloat16)
    d_normed = jnp.einsum("ijf,kf->ijk", d_hidden, trans_up, preferred_element_type=jnp.float32)
    scaled = d_normed * ln_gain
    d_middle = pair_cot.astype(jnp.float32) + inverse * (
        scaled
        - jnp.mean(scaled, axis=-1, keepdims=True)
        - normal_x * jnp.mean(scaled * normal_x, axis=-1, keepdims=True)
    )
    d_middle = d_middle.astype(jnp.bfloat16)
    d_outer = jnp.einsum("ijk,ck->ijc", d_middle, out_weight, preferred_element_type=jnp.float32)
    return (pair_out, d_outer.astype(jnp.bfloat16))


def on_device(left, right, pair_in, pair_cot, ln_gain, out_weight, out_bias, trans_up, trans_down):
    row_count = pair_in.shape[0]
    col_count = pair_in.shape[1]
    left_all = lax.all_gather(left, "col", axis=0, tiled=True)
    left_rows = left_all.reshape(SEQS, row_count, C)
    right_all = collect(right, "row", 0)
    summed = jnp.einsum(
        "sic,sje->ijce",
        left_rows,
        right_all.reshape(SEQS, col_count, C),
        preferred_element_type=jnp.float32,
    )
    outer = (summed * (1.0 / SEQS)).astype(jnp.bfloat16).reshape(row_count, col_count, C * C)
    pair_out, d_outer = pair_block(
        outer, pair_in, pair_cot, ln_gain, out_weight, out_bias, trans_up, trans_down
    )
    grad_tiles = d_outer.reshape(row_count, col_count, C, C)
    right_cols = right_all.reshape(SEQS, col_count, C)
    product = jnp.einsum("ijce,sic->sje", grad_tiles, left_rows, preferred_element_type=jnp.float32)
    right_total = sum_at_owner(
        product.reshape(right.shape[0] * lax.axis_size("row"), col_count * C).astype(jnp.bfloat16),
        "row",
        0,
    )
    product = jnp.einsum(
        "ijce,sje->sic", grad_tiles, right_cols, preferred_element_type=jnp.float32
    )
    left_total = sum_at_owner(
        product.reshape(left.shape[0] * lax.axis_size("col"), row_count * C).astype(jnp.bfloat16),
        "col",
        0,
    )
    grad_left = (left_total * (1.0 / SEQS)).astype(jnp.bfloat16)
    grad_right = (right_total * (1.0 / SEQS)).astype(jnp.bfloat16)
    return (pair_out, grad_left, grad_right)


def solution(mesh):
    return jax.shard_map(
        on_device,
        mesh=mesh,
        in_specs=(
            P("col", "row"),
            P("row", "col"),
            P("row", "col", None),
            P("row", "col", None),
            P(),
            P(),
            P(),
            P(),
            P(),
        ),
        out_specs=(P("row", "col", None), P("col", "row"), P("row", "col")),
        check_vma=False,
    )
```

profile of v0, /device:TPU:1, one launch (start us, length us, event | category | flops | bytes accessed | tf_op | source)
XLA Modules:
  0.0 121.9 jit_solution(1447077234070717280)
XLA Ops:
  0.6 1.5 %broadcast_in_dim.3 = bf16[32,4,1024]{2,1,0:T(4,128)(2,1)} broadcast(bf16[4,1024]{1,0:T(4,128)(2,1)} %param.10), dimensions={1,2} | broadcast | bytes 270336 | tf_op jit(solution)/shard_map/broadcast_in_dim | solution.py:17
  2.1 18.5 %all-to-all-start = ((bf16[32,4,1024]{2,1,0:T(4,128)(2,1)}), bf16[32,4,1024]{2,1,0:T(4,128)(2,1)S(1)}, u32[]{:S(2)}, u32[]{:S(2)}) async-start(bf16[32,4,1024]{2,1,0:T(4,128)(2,1)} %broadcast_in_dim.3), calls=%async_computation | async-start | bytes 524288 | tf_op jit(solution)/shard_map/all_to_all | solution.py:18
  20.6 20.5 %all_gather.3 = bf16[128,512]{1,0:T(8,128)(2,1)S(1)} all-gather(bf16[8,512]{1,0:T(8,128)(2,1)} %param.9), channel_id=1, replica_groups=mesh['row'=32,'col'=16] {'col'}, dimensions={0}, use_global_device_ids=true | all-gather | bytes 139264 | tf_op jit(solution)/shard_map/all_gather | solution.py:66
  41.3 0.9 all-to-all-done
  42.1 0.6 reshape_reshape.4
  42.7 4.5 %fusion = bf16[16,32,32,32]{2,3,0,1:T(8,128)(2,1)} fusion(bf16[128,16,32,1]{0,2,1,3:T(8,128)(2,1)S(1)} %bitcast.60, bf16[128,32,32,1]{2,1,0,3:T(8,128)(2,1)S(1)} %bitcast.58), kind=kOutput, calls=%fused_computation.1 | convolution fusion | flops 135266304 | bytes 1441792 | tf_op jit(solution)/shard_map/sic,sje->ijce/dot_general | solution.py:69
  47.2 6.4 %copy.19 = bf16[16,32,32,32]{3,2,1,0:T(8,128)(2,1)} copy(bf16[16,32,32,32]{2,3,0,1:T(8,128)(2,1)} %fusion) | data formatting | bytes 2097152 | tf_op jit(solution)/shard_map/convert_element_type | solution.py:75
  53.6 6.2 %reshape.46 = bf16[16,32,1024]{2,1,0:T(8,128)(2,1)S(1)} reshape(bf16[16,32,32,32]{3,2,1,0:T(8,128)(2,1)} %copy.19) | data formatting | bytes 2097152 | tf_op jit(solution)/shard_map/reshape | solution.py:75
  59.8 0.5 fusion.33
  60.6 1.3 %fusion.12 = (u16[32,512]{1,0:T(8,128)(2,1)S(1)}, bf16[16,32,512]{2,1,0:T(8,128)(2,1)S(1)}) fusion(bf16[128,512]{1,0:T(8,128)(2,1)} %param.16, f32[16,32,128]{2,1,0:T(8,128)S(1)} %get-tuple-element.6, f32[128]{0:T(128)} %param.13, f32[16,32]{1,0:T(8,128)S(1)} %add_rsqrt_fusion, f32[16,32]{1,0:T(8,128)S(1)} %broadcast_multiply_fusion.2), kind=kOutput, calls=%fused_computation.22 | convolution fusion | flops 68927488 | bytes 954880 | tf_op jit(solution)/shard_map/ijk,kf->ijf/dot_general | solution.py:45
  62.2 1.5 %fusion.32 = (f32[16,32]{1,0:T(8,128)S(1)}, f32[16,32]{1,0:T(8,128)S(1)}, f32[16,32,128]{2,1,0:T(8,128)S(1)}) fusion(f32[16,32]{1,0:T(8,128)S(1)} %add_rsqrt_fusion, f32[16,32,128]{2,1,0:T(8,128)S(1)} %get-tuple-element.6, f32[16,32]{1,0:T(8,128)S(1)} %broadcast_multiply_fusion.2, f32[128]{0:T(128)} %param.13, bf16[128,512]{1,0:T(8,128)(2,1)} %param.16, ...), kind=kOutput, calls=%fused_computation.54 | convolution fusion | flops 135134208 | bytes 1188352 | tf_op jit(solution)/shard_map/ijf,kf->ijk/dot_general | solution.py:51
  63.8 1.5 %convolution_convert_fusion = bf16[16,32,1024]{2,1,0:T(8,128)(2,1)S(1)} fusion(bf16[1024,128]{1,0:T(8,128)(2,1)S(1)} %copy-done, f32[16,32,128]{2,1,0:T(8,128)S(1)} %get-tuple-element.9, bf16[16,32,128]{2,1,0:T(8,128)(2,1)} %param.12, f32[16,32,128]{2,1,0:T(8,128)S(1)} %get-tuple-element.6, f32[16,32]{1,0:T(8,128)S(1)} %get-tuple-element.10, ...), kind=kOutput, calls=%fused_computation.2 | convolution fusion | flops 135331840 | bytes 1974272 | tf_op jit(solution)/shard_map/ijk,ck->ijc/dot_general | solution.py:59
  65.3 4.4 %reshape.47 = bf16[16,32,32,32]{3,2,1,0:T(8,128)(2,1)} reshape(bf16[16,32,1024]{2,1,0:T(8,128)(2,1)S(1)} %convolution_convert_fusion) | data formatting | bytes 2097152 | tf_op jit(solution)/shard_map/reshape | solution.py:79
  69.7 3.4 %fusion.9 = bf16[128,16,32]{0,2,1:T(8,128)(2,1)S(1)} fusion(bf16[16,32,32,32]{3,2,1,0:T(8,128)(2,1)} %reshape.47, bf16[128,32,32,1]{2,1,0,3:T(8,128)(2,1)S(1)} %bitcast.59), kind=kOutput, calls=%fused_computation.16 | convolution fusion | flops 134283264 | bytes 1441792 | tf_op jit(solution)/shard_map/ijce,sje->sic/dot_general | solution.py:87
  73.6 1.1 convert_element_type.74
  74.7 7.8 %all-to-all-start.1 = ((bf16[16,8,512]{2,1,0:T(8,128)(2,1)}), bf16[16,8,512]{2,1,0:T(8,128)(2,1)S(1)}, u32[]{:S(2)}, u32[]{:S(2)}) async-start(bf16[16,8,512]{2,1,0:T(8,128)(2,1)} %convert_element_type.74), calls=%async_computation.1 | async-start | bytes 262144 | tf_op jit(solution)/shard_map/all_to_all | solution.py:32
  82.5 3.4 %fusion.4 = bf16[128,32,32]{0,2,1:T(8,128)(2,1)S(1)} fusion(bf16[16,32,32,32]{3,2,1,0:T(8,128)(2,1)} %reshape.47, bf16[128,16,32,1]{0,2,3,1:T(8,128)(2,1)S(1)} %bitcast.61), kind=kOutput, calls=%fused_computation.8 | convolution fusion | flops 134348800 | bytes 1441792 | tf_op jit(solution)/shard_map/ijce,sic->sje/dot_general | solution.py:81
  85.9 1.5 %copy.24 = bf16[128,32,32]{2,1,0:T(8,128)(2,1)S(1)} copy(bf16[128,32,32]{0,2,1:T(8,128)(2,1)S(1)} %fusion.4) | data formatting | bytes 524288 | tf_op jit(solution)/shard_map/convert_element_type | solution.py:83
  87.4 1.7 %convert_element_type.79 = bf16[32,4,1024]{2,1,0:T(4,128)(2,1)} reshape(bf16[128,32,32]{2,1,0:T(8,128)(2,1)S(1)} %copy.24) | data formatting | bytes 524288 | tf_op jit(solution)/shard_map/convert_element_type | solution.py:83
  89.1 10.0 %all-to-all-start.2 = ((bf16[32,4,1024]{2,1,0:T(4,128)(2,1)}), bf16[32,4,1024]{2,1,0:T(4,128)(2,1)S(1)}, u32[]{:S(2)}, u32[]{:S(2)}) async-start(bf16[32,4,1024]{2,1,0:T(4,128)(2,1)} %convert_element_type.79), calls=%async_computation.2 | async-start | bytes 524288 | tf_op jit(solution)/shard_map/all_to_all | solution.py:32
  99.2 1.0 fusion.7
  100.2 0.6 multiply_convert_fusion.4
  100.8 20.4 %all-to-all-done.2 = bf16[32,4,1024]{2,1,0:T(4,128)(2,1)S(1)} async-done(((bf16[32,4,1024]{2,1,0:T(4,128)(2,1)}), bf16[32,4,1024]{2,1,0:T(4,128)(2,1)S(1)}, u32[]{:S(2)}, u32[]{:S(2)}) %all-to-all-start.2) | async-done | bytes 262176 | tf_op jit(solution)/shard_map/all_to_all | solution.py:32
  121.3 0.6 multiply_convert_fusion.3
  (22 shorter events, 1.3 us)
Async XLA Ops:
  0.6 59.2 %copy-start = (bf16[1024,128]{1,0:T(8,128)(2,1)S(1)}, bf16[1024,128]{1,0:T(8,128)(2,1)}, u32[]{:S(2)}) copy-start(bf16[1024,128]{1,0:T(8,128)(2,1)} %param.14) | copy-start | bytes 786436
  2.1 40.0 %all-to-all-start = ((bf16[32,4,1024]{2,1,0:T(4,128)(2,1)}), bf16[32,4,1024]{2,1,0:T(4,128)(2,1)S(1)}, u32[]{:S(2)}, u32[]{:S(2)}) async-start(bf16[32,4,1024]{2,1,0:T(4,128)(2,1)} %broadcast_in_dim.3), calls=%async_computation | async-start | bytes 524288 | tf_op jit(solution)/shard_map/all_to_all | solution.py:18
  53.6 6.3 %copy-start.1 = (bf16[16,32,128]{2,1,0:T(8,128)(2,1)S(1)}, bf16[16,32,128]{2,1,0:T(8,128)(2,1)}, u32[]{:S(2)}) copy-start(bf16[16,32,128]{2,1,0:T(8,128)(2,1)} %param.11) | copy-start | bytes 393220
  53.6 6.3 %copy-start.5 = (f32[128]{0:T(128)S(1)}, f32[128]{0:T(128)}, u32[]{:S(2)}) copy-start(f32[128]{0:T(128)} %param.15) | copy-start | bytes 1540
  53.6 8.6 %copy-start.2 = (bf16[512,128]{1,0:T(8,128)(2,1)S(1)}, bf16[512,128]{1,0:T(8,128)(2,1)}, u32[]{:S(2)}) copy-start(bf16[512,128]{1,0:T(8,128)(2,1)} %param.17) | copy-start | bytes 393220
  53.6 8.7 %copy-start.4 = (bf16[16,32,128]{2,1,0:T(8,128)(2,1)S(1)}, bf16[16,32,128]{2,1,0:T(8,128)(2,1)}, u32[]{:S(2)}) copy-start(bf16[16,32,128]{2,1,0:T(8,128)(2,1)} %param.12) | copy-start | bytes 393220
  74.7 24.5 %copy-start.3 = (bf16[512,128]{1,0:T(8,128)(2,1)S(1)}, bf16[512,128]{1,0:T(8,128)(2,1)}, u32[]{:S(2)}) copy-start(bf16[512,128]{1,0:T(8,128)(2,1)} %param.17) | copy-start | bytes 393220
  74.7 14.5 %all-to-all-start.1 = ((bf16[16,8,512]{2,1,0:T(8,128)(2,1)}), bf16[16,8,512]{2,1,0:T(8,128)(2,1)S(1)}, u32[]{:S(2)}, u32[]{:S(2)}) async-start(bf16[16,8,512]{2,1,0:T(8,128)(2,1)} %convert_element_type.74), calls=%async_computation.1 | async-start | bytes 262144 | tf_op jit(solution)/shard_map/all_to_all | solution.py:32
  89.1 32.0 %all-to-all-start.2 = ((bf16[32,4,1024]{2,1,0:T(4,128)(2,1)}), bf16[32,4,1024]{2,1,0:T(4,128)(2,1)S(1)}, u32[]{:S(2)}, u32[]{:S(2)}) async-start(bf16[32,4,1024]{2,1,0:T(4,128)(2,1)} %convert_element_type.79), calls=%async_computation.2 | async-start | bytes 524288 | tf_op jit(solution)/shard_map/all_to_all | solution.py:32
where the time goes:
time: 124 us; the launch traced here: 122 us
  starting transfers between devices  36.3 us (29%)
  local copies, waits for them, and re-layouts  23.9 us (19%)
  waiting for transfers between devices  21.2 us (17%)
  blocking collectives  20.5 us (17%)
  matrix products  17.2 us (14%)
  other arithmetic  1.89 us (2%)
    all_gather x1, blocking collectives, on_device(): left_all = lax.all_gather(left, 'col', axis=0, tiled=True)  20.5 us
    all_to_all x2, waiting for transfers between devices, sum_at_owner(): lax.all_to_all(tiles, axis, split_axis=0, concat_axis=0, tiled=True)  20.4 us
    all_to_all x1, starting transfers between devices, sent_to_all(): return lax.all_to_all(copies, axis, split_axis=0, concat_axis=0, tiled=True)  18.5 us
    all_to_all x2, starting transfers between devices, sum_at_owner(): lax.all_to_all(tiles, axis, split_axis=0, concat_axis=0, tiled=True)  17.9 us
    convert_element_type x1, local copies, waits for them, and re-layouts, on_device(): (summed * (1.0 / SEQS)).astype(jnp.bfloat16)  6.35 us
    reshape x1, local copies, waits for them, and re-layouts, on_device(): (summed * (1.0 / SEQS)).astype(jnp.bfloat16)  6.22 us
    dot_general x1, matrix products, on_device(): jnp.einsum('sic,sje->ijce', left_rows, right_all.reshape(SEQS, col_count,...  4.48 us
    reshape x1, local copies, waits for them, and re-layouts, on_device(): grad_tiles = d_outer.reshape(row_count, col_count, C, C)  4.37 us
  transfers between devices with their start and end apart: 3, of which 2 were waited for; matrix products, arithmetic and copies ran while one was open for 7% of the time, Pallas kernels for 0%

commit v1 on v0

v1 whole, which is shorter than its diff:
```python
import jax
import jax.numpy as jnp
from jax import lax
from jax.experimental import pallas as pl
from jax.experimental.pallas import tpu as pltpu
from jax.sharding import PartitionSpec as P

C = 32
SEQS = 128
GROUPS = 128 // C
F32 = jnp.float32
BF16 = jnp.bfloat16
NN = (((1,), (0,)), ((), ()))
NT = (((1,), (1,)), ((), ()))
TN = (((0,), (0,)), ((), ()))


def mm(a, b, dims=NN):
    return lax.dot_general(a, b, dims, preferred_element_type=F32)


def swap_rows(major, minor):
    n = major * minor
    row = lax.broadcasted_iota(jnp.int32, (n, n), 0)
    col = lax.broadcasted_iota(jnp.int32, (n, n), 1)
    return jnp.where(col == (row % minor) * major + row // minor, 1.0, 0.0).astype(BF16)


def exchange(tiles):
    axis = tiles[0].ndim - 1
    lane = lax.broadcasted_iota(jnp.int32, tiles[0].shape, axis)
    low, even = lane < 64, lane % 64 < 32
    a0, a1, a2, a3 = tiles
    b0, b2 = jnp.where(low, a0, pltpu.roll(a2, 64, axis)), jnp.where(low, pltpu.roll(a0, 64, axis), a2)
    b1, b3 = jnp.where(low, a1, pltpu.roll(a3, 64, axis)), jnp.where(low, pltpu.roll(a1, 64, axis), a3)
    c0, c1 = jnp.where(even, b0, pltpu.roll(b1, 32, axis)), jnp.where(even, pltpu.roll(b0, 96, axis), b1)
    c2, c3 = jnp.where(even, b2, pltpu.roll(b3, 32, axis)), jnp.where(even, pltpu.roll(b2, 96, axis), b3)
    return c0, c1, c2, c3


def regroup(src, dst, rows, scale=None):
    for g in range(src.shape[0] // (GROUPS * rows)):
        for h in range(src.shape[1] // 128):
            tiles = [
                src[(GROUPS * g + t) * rows : (GROUPS * g + t + 1) * rows, h * 128 : (h + 1) * 128]
                for t in range(GROUPS)
            ]
            if scale is not None:
                tiles = [tile * scale for tile in tiles]
            for t, tile in enumerate(exchange(tiles)):
                at = (GROUPS * h + t) * rows
                dst[at : at + rows, g * 128 : (g + 1) * 128] = tile.astype(dst.dtype)


def prepare(left, pair_in, pair_cot, down, left_t, left_p, pair_p, cot_p, back):
    rows, cols, _ = pair_in.shape
    swap = swap_rows(C, rows)
    swap_pair = swap if cols == C else swap_rows(cols, rows)
    left_t[...] = mm(swap, left[...], NT).astype(BF16)
    left_p[...] = mm(left[...], swap, NT).astype(BF16)
    pair_p[...] = mm(swap_pair, pair_in[...].reshape(rows * cols, -1)).astype(BF16)
    cot = mm(swap_pair, pair_cot[...].reshape(rows * cols, -1)).astype(BF16)
    cot_p[...] = cot
    back[...] = mm(cot, down[...], NT).astype(BF16)


def pair_step(
    right, left_t, left_p, pair_p, cot_p, back, gain, weight, bias, up,
    grad_right, right_all, d_tiles, middle_out, hidden_out,
    tall, outer,
):
    owners, each, width = right.shape
    rows = left_t.shape[0] // C
    for k in range(owners):
        tall[k * each : (k + 1) * each, :] = right[k].astype(F32)
    right_all[...] = tall[: owners * each, :].astype(BF16)
    tall[...] = mm(left_t[...], right_all[...])
    regroup(tall, outer, rows, 1.0 / SEQS)
    middle = pair_p[...].astype(F32) + mm(outer[...], weight[...]) + bias[...]
    middle_out[...] = middle
    centre = jnp.mean(middle, axis=-1, keepdims=True)
    centred = middle - centre
    spread = jnp.mean(centred * centred, axis=-1, keepdims=True)
    inverse = lax.rsqrt(spread + 1e-05)
    normal_x = centred * inverse
    normed = (normal_x * gain[...]).astype(BF16)
    preact = mm(normed, up[...])
    hidden_out[...] = jnp.maximum(preact, 0.0).astype(BF16)
    d_hidden = jnp.where(preact > 0.0, back[...].astype(F32), 0.0).astype(BF16)
    scaled = mm(d_hidden, up[...], NT) * gain[...]
    d_middle = cot_p[...].astype(F32) + inverse * (
        scaled
        - jnp.mean(scaled, axis=-1, keepdims=True)
        - normal_x * jnp.mean(scaled * normal_x, axis=-1, keepdims=True)
    )
    tall[...] = mm(d_middle.astype(BF16), weight[...], NT)
    regroup(tall, d_tiles, rows)
    tall[: owners * each, :] = mm(left_p[...], d_tiles[...])
    for k in range(owners):
        grad_right[k] = tall[k * each : (k + 1) * each, :].astype(BF16)


def finish(right_all, d_tiles, middle, hidden, down, grad_left, pair_out):
    rows, cols, _ = pair_out.shape
    swap = swap_rows(C, rows)
    swap_pair = swap if cols == C else swap_rows(cols, rows)
    partial = mm(right_all[...], d_tiles[...], NT).astype(BF16)
    grad_left[...] = mm(partial, swap).astype(BF16)
    out = (middle[...] + mm(hidden[...], down[...])).astype(BF16)
    pair_out[...] = mm(swap_pair, out, TN).astype(BF16).reshape(pair_out.shape)


def on_core(kernel, outs, scratch=()):
    whole = pl.BlockSpec(memory_space=pltpu.VMEM)

    def run(*args):
        return pl.pallas_call(
            kernel,
            out_shape=[jax.ShapeDtypeStruct(*out) for out in outs],
            in_specs=[whole] * len(args),
            out_specs=[whole] * len(outs),
            scratch_shapes=[pltpu.VMEM(*s) for s in scratch],
            compiler_params=pltpu.CompilerParams(vmem_limit_bytes=32 << 20),
            cost_estimate=pl.CostEstimate(
                flops=400_000_000, bytes_accessed=2_000_000, transcendentals=0
            ),
        )(*args)

    return run


def sent_to_all(shard, axis):
    copies = jnp.broadcast_to(shard, (lax.axis_size(axis), *shard.shape))
    return lax.all_to_all(copies, axis, split_axis=0, concat_axis=0, tiled=True)


def sum_at_owner(tiles, axis):
    arrived = lax.all_to_all(tiles, axis, split_axis=0, concat_axis=0, tiled=True)
    return (arrived.astype(F32).sum(axis=0) * (1.0 / SEQS)).astype(BF16)


def on_device(left, right, pair_in, pair_cot, ln_gain, out_weight, out_bias, trans_up, trans_down):
    rows, cols, dim = pair_in.shape
    cells, ffn = rows * cols, trans_up.shape[1]
    right_blocks = sent_to_all(right, "row")
    left_all = lax.all_gather(left, "col", axis=0, tiled=True)
    left_t, left_p, pair_p, cot_p, back = on_core(
        prepare,
        [
            ((rows * C, SEQS), BF16),
            ((SEQS, rows * C), BF16),
            ((cells, dim), BF16),
            ((cells, dim), BF16),
            ((cells, ffn), BF16),
        ],
    )(left_all, pair_in, pair_cot, trans_down)
    grad_right, right_all, d_tiles, middle, hidden = on_core(
        pair_step,
        [
            (right_blocks.shape, BF16),
            ((SEQS, cols * C), BF16),
            ((rows * C, cols * C), BF16),
            ((cells, dim), F32),
            ((cells, ffn), BF16),
        ],
        [((max(rows * C, cells), cols * C), F32), ((cells, C * C), BF16)],
    )(
        right_blocks, left_t, left_p, pair_p, cot_p, back,
        ln_gain.reshape(1, dim), out_weight, out_bias.reshape(1, dim), trans_up,
    )
    grad_right = sum_at_owner(grad_right, "row")
    grad_left, pair_out = on_core(
        finish, [((SEQS, rows * C), BF16), (pair_in.shape, BF16)]
    )(right_all, d_tiles, middle, hidden, trans_down)
    grad_left = sum_at_owner(grad_left.reshape(-1, *left.shape), "col")
    return pair_out, grad_left, grad_right


def solution(mesh):
    return jax.shard_map(
        on_device,
        mesh=mesh,
        in_specs=(
            P("col", "row"),
            P("row", "col"),
            P("row", "col", None),
            P("row", "col", None),
            P(),
            P(),
            P(),
            P(),
            P(),
        ),
        out_specs=(P("row", "col", None), P("col", "row"), P("row", "col")),
        check_vma=False,
    )
```

time: 124 us -> 95.8 us (0.77)
  local copies, waits for them, and re-layouts: 23.9 us -> 2.16 us
  matrix products: 17.2 us -> 0 us
  blocking collectives: 20.5 us -> 34.1 us
  starting transfers between devices: 36.3 us -> 28.6 us
  Pallas kernels: 0 us -> 6.95 us
    dot_general x8 -> x0, matrix products: 17.2 us -> none  [the longest x1 4.48 us: on_device(): jnp.einsum('sic,sje->ijce', left_rows, right_all.reshape(SEQS, col_count,...]
    all_to_all x0 -> x1, blocking collectives: none -> 13.6 us  [sum_at_owner(): lax.all_to_all(tiles, axis, split_axis=0, concat_axis=0, tiled=True)]
    convert_element_type x5 -> x0, local copies, waits for them, and re-layouts: 11.1 us -> none  [the longest x1 6.35 us: on_device(): (summed * (1.0 / SEQS)).astype(jnp.bfloat16)]
    reshape x2 -> x0, local copies, waits for them, and re-layouts: 10.6 us -> none  [the longest x1 6.22 us: on_device(): (summed * (1.0 / SEQS)).astype(jnp.bfloat16)]
    all_to_all x2 -> x1, starting transfers between devices: 17.9 us -> 9.99 us  [sum_at_owner(): lax.all_to_all(tiles, axis, split_axis=0, concat_axis=0, tiled=True)]
    pallas_call x0 -> x3, Pallas kernels: none -> 6.95 us  [run(): pl.pallas_call(kernel, out_shape=[jax.ShapeDtypeStruct(*out) for out in o...]
    all_to_all x2 -> x1, waiting for transfers between devices: 20.4 us -> 20.9 us  [sum_at_owner(): lax.all_to_all(tiles, axis, split_axis=0, concat_axis=0, tiled=True)]
  transfers between devices with their start and end apart: 3 -> 2, of which waited for: 2 -> 2; matrix products, arithmetic and copies ran while one was open for 7% -> 1% of each run, Pallas kernels for 0% -> 1%
where the time goes in v1:
time: 95.8 us; the launch traced here: 94.9 us
  blocking collectives  34.1 us (36%)
  starting transfers between devices  28.6 us (30%)
  waiting for transfers between devices  21 us (22%)
  Pallas kernels  6.95 us (7%)
  local copies, waits for them, and re-layouts  2.16 us (2%)
  other arithmetic  1.36 us (1%)
    all_to_all x1, waiting for transfers between devices, sum_at_owner(): lax.all_to_all(tiles, axis, split_axis=0, concat_axis=0, tiled=True)  20.9 us
    all_gather x1, blocking collectives, on_device(): left_all = lax.all_gather(left, 'col', axis=0, tiled=True)  20.4 us
    all_to_all x1, starting transfers between devices, sent_to_all(): return lax.all_to_all(copies, axis, split_axis=0, concat_axis=0, tiled=True)  18.6 us
    all_to_all x1, blocking collectives, sum_at_owner(): lax.all_to_all(tiles, axis, split_axis=0, concat_axis=0, tiled=True)  13.6 us
    all_to_all x1, starting transfers between devices, sum_at_owner(): lax.all_to_all(tiles, axis, split_axis=0, concat_axis=0, tiled=True)  9.99 us
    pallas_call x3, Pallas kernels, run(): pl.pallas_call(kernel, out_shape=[jax.ShapeDtypeStruct(*out) for out in o...  6.95 us
  transfers between devices with their start and end apart: 2, of which 2 were waited for; matrix products, arithmetic and copies ran while one was open for 1% of the time, Pallas kernels for 1%

profile of v1, /device:TPU:1, one launch (start us, length us, event | category | flops | bytes accessed | tf_op | source)
XLA Modules:
  0.0 94.9 jit_solution(2934992223044488896)
XLA Ops:
  0.6 1.5 %broadcast_in_dim.3 = bf16[32,4,1024]{2,1,0:T(4,128)(2,1)} broadcast(bf16[4,1024]{1,0:T(4,128)(2,1)} %param.10), dimensions={1,2} | broadcast | bytes 270336 | tf_op jit(solution)/shard_map/broadcast_in_dim | solution.py:133
  2.1 18.6 %all-to-all-start = ((bf16[32,4,1024]{2,1,0:T(4,128)(2,1)}), bf16[32,4,1024]{2,1,0:T(4,128)(2,1)S(1)}, u32[]{:S(2)}, u32[]{:S(2)}) async-start(bf16[32,4,1024]{2,1,0:T(4,128)(2,1)} %broadcast_in_dim.3), calls=%async_computation | async-start | bytes 524288 | tf_op jit(solution)/shard_map/all_to_all | solution.py:134
  20.7 0.0 copy-done.7
  20.7 0.0 copy-start.2
  20.8 20.4 %all_gather.3.left = bf16[128,512]{1,0:T(8,128)(2,1)S(1)} all-gather(bf16[8,512]{1,0:T(8,128)(2,1)S(1)} %copy-done.7), channel_id=1, replica_groups=mesh['row'=32,'col'=16] {'col'}, dimensions={0}, use_global_device_ids=true | all-gather | bytes 139264 | tf_op jit(solution)/shard_map/all_gather | solution.py:146
  41.2 0.0 copy-done.5
  41.2 0.0 copy-done.6
  41.2 0.0 copy-done.2
  41.2 0.0 copy-start
  41.2 0.0 copy-start.1
  41.2 0.9 shard_map.112
  42.1 0.1 all-to-all-done.right
  42.2 0.0 copy-done
  42.2 0.0 copy-done.1
  42.2 0.6 copy-done.3
  42.9 0.0 copy-done.4
  42.9 4.2 %shard_map.113 = (bf16[32,4,1024]{2,1,0:T(4,128)(2,1)}, bf16[128,1024]{1,0:T(8,128)(2,1)S(1)}, bf16[512,1024]{1,0:T(8,128)(2,1)S(1)}, f32[512,128]{1,0:T(8,128)S(1)}, bf16[512,512]{1,0:T(8,128)(2,1)S(1)}) custom-call(bf16[32,4,1024]{2,1,0:T(4,128)(2,1)S(1)} %all-to-all-done.right, bf16[512,128]{1,0:T(8,128)(2,1)S(1)} %get-tuple-element.15.left_t, ...), custom_call_target="tpu_custom_call" | custom-call | flops 400000000 | bytes 2000000 | tf_op jit(solution)/shard_map/pallas_call | solution.py:117
  47.1 1.9 %shard_map.114 = (bf16[128,512]{1,0:T(8,128)(2,1)S(1)}, bf16[16,32,128]{2,1,0:T(8,128)(2,1)}) custom-call(bf16[128,1024]{1,0:T(8,128)(2,1)S(1)} %get-tuple-element.20.right_all, bf16[512,1024]{1,0:T(8,128)(2,1)S(1)} %get-tuple-element.21.d_tiles, f32[512,128]{1,0:T(8,128)S(1)} %get-tuple-element.22.middle, bf16[512,512]{1,0:T(8,128)(2,1)S(1)} %get-tuple-element.23.hidden, ...), custom_call_target="tpu_custom_call" | custom-call | flops 400000000 | bytes 2000000 | tf_op jit(solution)/shard_map/pallas_call | solution.py:117
  49.0 13.6 %all_to_all.15 = bf16[16,8,512]{2,1,0:T(8,128)(2,1)S(1)} all-to-all(bf16[16,8,512]{2,1,0:T(8,128)(2,1)S(1)} %bitcast.3), channel_id=1, replica_groups=mesh['row'=32,'col'=16] {'col'}, dimensions={0} | all-to-all | bytes 262144 | tf_op jit(solution)/shard_map/all_to_all | solution.py:138
  62.6 10.0 %all-to-all-start.2 = ((bf16[32,4,1024]{2,1,0:T(4,128)(2,1)}), bf16[32,4,1024]{2,1,0:T(4,128)(2,1)S(1)}, u32[]{:S(2)}, u32[]{:S(2)}) async-start(bf16[32,4,1024]{2,1,0:T(4,128)(2,1)} %get-tuple-element.26), calls=%async_computation.2 | async-start | bytes 524288 | tf_op jit(solution)/shard_map/all_to_all | solution.py:138
  72.7 0.6 multiply_convert_fusion.1
  73.3 20.9 %all-to-all-done.2 = bf16[32,4,1024]{2,1,0:T(4,128)(2,1)S(1)} async-done(((bf16[32,4,1024]{2,1,0:T(4,128)(2,1)}), bf16[32,4,1024]{2,1,0:T(4,128)(2,1)S(1)}, u32[]{:S(2)}, u32[]{:S(2)}) %all-to-all-start.2) | async-done | bytes 262176 | tf_op jit(solution)/shard_map/all_to_all | solution.py:138
  94.1 0.1 convert_reduce_fusion
  94.3 0.6 multiply_convert_fusion
  (6 shorter events, 0.0 us)
Async XLA Ops:
  2.1 18.6 %copy-start.7 = (bf16[8,512]{1,0:T(8,128)(2,1)S(1)}, bf16[8,512]{1,0:T(8,128)(2,1)}, u32[]{:S(2)}) copy-start(bf16[8,512]{1,0:T(8,128)(2,1)} %param.9) | copy-start | bytes 24580
  2.1 39.1 %copy-start.5 = (bf16[16,32,128]{2,1,0:T(8,128)(2,1)S(1)}, bf16[16,32,128]{2,1,0:T(8,128)(2,1)}, u32[]{:S(2)}) copy-start(bf16[16,32,128]{2,1,0:T(8,128)(2,1)} %pair_in.1) | copy-start | bytes 393220
  2.1 39.1 %copy-start.6 = (bf16[16,32,128]{2,1,0:T(8,128)(2,1)S(1)}, bf16[16,32,128]{2,1,0:T(8,128)(2,1)}, u32[]{:S(2)}) copy-start(bf16[16,32,128]{2,1,0:T(8,128)(2,1)} %pair_cot.1) | copy-start | bytes 393220
  2.1 40.1 %all-to-all-start = ((bf16[32,4,1024]{2,1,0:T(4,128)(2,1)}), bf16[32,4,1024]{2,1,0:T(4,128)(2,1)S(1)}, u32[]{:S(2)}, u32[]{:S(2)}) async-start(bf16[32,4,1024]{2,1,0:T(4,128)(2,1)} %broadcast_in_dim.3), calls=%async_computation | async-start | bytes 524288 | tf_op jit(solution)/shard_map/all_to_all | solution.py:134
  20.7 20.5 %copy-start.2 = (bf16[512,128]{1,0:T(8,128)(2,1)S(1)}, bf16[512,128]{1,0:T(8,128)(2,1)}, u32[]{:S(2)}) copy-start(bf16[512,128]{1,0:T(8,128)(2,1)} %down.3) | copy-start | bytes 393220
  41.2 1.0 %copy-start = (bf16[1024,128]{1,0:T(8,128)(2,1)S(1)}, bf16[1024,128]{1,0:T(8,128)(2,1)}, u32[]{:S(2)}) copy-start(bf16[1024,128]{1,0:T(8,128)(2,1)} %weight.1) | copy-start | bytes 786436
  41.2 1.0 %copy-start.1 = (bf16[128,512]{1,0:T(8,128)(2,1)S(1)}, bf16[128,512]{1,0:T(8,128)(2,1)}, u32[]{:S(2)}) copy-start(bf16[128,512]{1,0:T(8,128)(2,1)} %up.1) | copy-start | bytes 393220
  42.2 0.7 copy-start.3
  42.2 0.7 copy-start.4
  62.6 31.5 %all-to-all-start.2 = ((bf16[32,4,1024]{2,1,0:T(4,128)(2,1)}), bf16[32,4,1024]{2,1,0:T(4,128)(2,1)S(1)}, u32[]{:S(2)}, u32[]{:S(2)}) async-start(bf16[32,4,1024]{2,1,0:T(4,128)(2,1)} %get-tuple-element.26), calls=%async_computation.2 | async-start | bytes 524288 | tf_op jit(solution)/shard_map/all_to_all | solution.py:138

commit v2 on v1

--- a/solution.py
+++ b/solution.py
@@ -52,7 +52,12 @@
                 dst[at : at + rows, g * 128 : (g + 1) * 128] = tile.astype(dst.dtype)
 
 
-def prepare(left, pair_in, pair_cot, down, left_t, left_p, pair_p, cot_p, back):
+def prepare(
+    left, pair_in, pair_cot, down, gain, bias,
+    left_t, left_p, pair_p, cot_p, back, gain_out, bias_out,
+):
+    gain_out[...] = gain[...]
+    bias_out[...] = bias[...]
     rows, cols, _ = pair_in.shape
     swap = swap_rows(C, rows)
     swap_pair = swap if cols == C else swap_rows(cols, rows)
@@ -66,7 +71,7 @@
 
 def pair_step(
     right, left_t, left_p, pair_p, cot_p, back, gain, weight, bias, up,
-    grad_right, right_all, d_tiles, middle_out, hidden_out,
+    away, kept, right_all, d_tiles, middle_out, hidden_out,
     tall, outer,
 ):
     owners, each, width = right.shape
@@ -95,17 +100,27 @@
     )
     tall[...] = mm(d_middle.astype(BF16), weight[...], NT)
     regroup(tall, d_tiles, rows)
-    tall[: owners * each, :] = mm(left_p[...], d_tiles[...])
+    half = SEQS // 2
+    mine = lax.axis_index("row") // (owners // 2)
+    away[...] = mm(left_p[pl.ds((1 - mine) * half, half), :], d_tiles[...]).astype(BF16)
+    kept[...] = mm(left_p[pl.ds(mine * half, half), :], d_tiles[...])
+
+
+def left_step(right_all, d_tiles, grad_left):
+    partial = mm(right_all[...], d_tiles[...], NT).astype(BF16)
+    grad_left[...] = mm(partial, swap_rows(C, grad_left.shape[1] // C)).astype(BF16)
+
+
+def join_halves(kept, came, tiles, total):
+    owners, each, _ = tiles.shape
+    total[...] = kept[...] + came[...].astype(F32)
     for k in range(owners):
-        grad_right[k] = tall[k * each : (k + 1) * each, :].astype(BF16)
-
-
-def finish(right_all, d_tiles, middle, hidden, down, grad_left, pair_out):
+        tiles[k] = total[k * each : (k + 1) * each, :].astype(BF16)
+
+
+def finish(middle, hidden, down, pair_out):
     rows, cols, _ = pair_out.shape
-    swap = swap_rows(C, rows)
-    swap_pair = swap if cols == C else swap_rows(cols, rows)
-    partial = mm(right_all[...], d_tiles[...], NT).astype(BF16)
-    grad_left[...] = mm(partial, swap).astype(BF16)
+    swap_pair = swap_rows(cols, rows)
     out = (middle[...] + mm(hidden[...], down[...])).astype(BF16)
     pair_out[...] = mm(swap_pair, out, TN).astype(BF16).reshape(pair_out.shape)
 
@@ -134,8 +149,10 @@
     return lax.all_to_all(copies, axis, split_axis=0, concat_axis=0, tiled=True)
 
 
-def sum_at_owner(tiles, axis):
-    arrived = lax.all_to_all(tiles, axis, split_axis=0, concat_axis=0, tiled=True)
+def sum_at_owner(tiles, axis, groups=None):
+    arrived = lax.all_to_all(
+        tiles, axis, split_axis=0, concat_axis=0, tiled=True, axis_index_groups=groups
+    )
     return (arrived.astype(F32).sum(axis=0) * (1.0 / SEQS)).astype(BF16)
 
 
@@ -144,7 +161,7 @@
     cells, ffn = rows * cols, trans_up.shape[1]
     right_blocks = sent_to_all(right, "row")
     left_all = lax.all_gather(left, "col", axis=0, tiled=True)
-    left_t, left_p, pair_p, cot_p, back = on_core(
+    left_t, left_p, pair_p, cot_p, back, gain, bias = on_core(
         prepare,
         [
             ((rows * C, SEQS), BF16),
@@ -152,27 +169,37 @@
             ((cells, dim), BF16),
             ((cells, dim), BF16),
             ((cells, ffn), BF16),
+            ((1, dim), F32),
+            ((1, dim), F32),
         ],
-    )(left_all, pair_in, pair_cot, trans_down)
-    grad_right, right_all, d_tiles, middle, hidden = on_core(
+    )(
+        left_all, pair_in, pair_cot, trans_down,
+        ln_gain.reshape(1, dim), out_bias.reshape(1, dim),
+    )
+    away, kept, right_all, d_tiles, middle, hidden = on_core(
         pair_step,
         [
-            (right_blocks.shape, BF16),
+            ((SEQS // 2, cols * C), BF16),
+            ((SEQS // 2, cols * C), F32),
             ((SEQS, cols * C), BF16),
             ((rows * C, cols * C), BF16),
             ((cells, dim), F32),
             ((cells, ffn), BF16),
         ],
         [((max(rows * C, cells), cols * C), F32), ((cells, C * C), BF16)],
-    )(
-        right_blocks, left_t, left_p, pair_p, cot_p, back,
-        ln_gain.reshape(1, dim), out_weight, out_bias.reshape(1, dim), trans_up,
-    )
-    grad_right = sum_at_owner(grad_right, "row")
-    grad_left, pair_out = on_core(
-        finish, [((SEQS, rows * C), BF16), (pair_in.shape, BF16)]
-    )(right_all, d_tiles, middle, hidden, trans_down)
+    )(right_blocks, left_t, left_p, pair_p, cot_p, back, gain, out_weight, bias, trans_up)
+    owners = lax.axis_size("row")
+    half = owners // 2
+    came = lax.ppermute(away, "row", [(k, (k + half) % owners) for k in range(owners)])
+    (grad_left,) = on_core(left_step, [((SEQS, rows * C), BF16)])(right_all, d_tiles)
     grad_left = sum_at_owner(grad_left.reshape(-1, *left.shape), "col")
+    (tiles,) = on_core(
+        join_halves, [((half, *right.shape), BF16)], [((SEQS // 2, cols * C), F32)]
+    )(kept, came)
+    grad_right = sum_at_owner(
+        tiles, "row", [list(range(half)), list(range(half, owners))]
+    )
+    (pair_out,) = on_core(finish, [(pair_in.shape, BF16)])(middle, hidden, trans_down)
     return pair_out, grad_left, grad_right
 
 

time: 95.8 us -> 89.1 us (0.930)
  the two profiles are of different devices: /device:TPU:1 before, /device:TPU:32 now
where the time goes in v2:
time: 89.1 us; the launch traced here: 88.6 us
  starting transfers between devices  37.8 us (42%)
  blocking collectives  19.6 us (22%)
  waiting for transfers between devices  19.5 us (22%)
  Pallas kernels  7.47 us (8%)
  local copies, waits for them, and re-layouts  2.15 us (2%)
  other arithmetic  1.3 us (1%)
    all_gather x1, blocking collectives, on_device(): left_all = lax.all_gather(left, 'col', axis=0, tiled=True)  19.6 us
    all_to_all x2, waiting for transfers between devices, sum_at_owner(): lax.all_to_all(tiles, axis, split_axis=0, concat_axis=0, tiled=True, axis...  18.2 us
    all_to_all x1, starting transfers between devices, sent_to_all(): return lax.all_to_all(copies, axis, split_axis=0, concat_axis=0, tiled=True)  17.9 us
    all_to_all x2, starting transfers between devices, sum_at_owner(): lax.all_to_all(tiles, axis, split_axis=0, concat_axis=0, tiled=True, axis...  15.6 us
    pallas_call x5, Pallas kernels, run(): pl.pallas_call(kernel, out_shape=[jax.ShapeDtypeStruct(*out) for out in o...  7.47 us
    ppermute x1, starting transfers between devices, on_device(): lax.ppermute(away, 'row', [(k, (k + half) % owners) for k in range(owners)])  4.25 us
  transfers between devices with their start and end apart: 4, of which 3 were waited for; matrix products, arithmetic and copies ran while one was open for 1% of the time, Pallas kernels for 5%

profile of v2, /device:TPU:32, one launch (start us, length us, event | category | flops | bytes accessed | tf_op | source)
XLA Modules:
  0.0 88.6 jit_solution(13947774774694550112)
XLA Ops:
  0.6 1.5 %broadcast_in_dim.3 = bf16[32,4,1024]{2,1,0:T(4,128)(2,1)} broadcast(bf16[4,1024]{1,0:T(4,128)(2,1)} %param.10), dimensions={1,2} | broadcast | bytes 270336 | tf_op jit(solution)/shard_map/broadcast_in_dim | solution.py:148
  2.1 17.9 %all-to-all-start = ((bf16[32,4,1024]{2,1,0:T(4,128)(2,1)}), bf16[32,4,1024]{2,1,0:T(4,128)(2,1)S(1)}, u32[]{:S(2)}, u32[]{:S(2)}) async-start(bf16[32,4,1024]{2,1,0:T(4,128)(2,1)} %broadcast_in_dim.3), calls=%async_computation | async-start | bytes 524288 | tf_op jit(solution)/shard_map/all_to_all | solution.py:149
  20.1 0.0 copy-done.7
  20.1 0.0 copy-start.2
  20.1 19.6 %all_gather.3.left = bf16[128,512]{1,0:T(8,128)(2,1)S(1)} all-gather(bf16[8,512]{1,0:T(8,128)(2,1)S(1)} %copy-done.7), channel_id=1, replica_groups=mesh['row'=32,'col'=16] {'col'}, dimensions={0}, use_global_device_ids=true | all-gather | bytes 139264 | tf_op jit(solution)/shard_map/all_gather | solution.py:163
  39.7 0.0 copy-done.3
  39.8 0.6 copy-done.5
  40.4 0.0 copy-done.6
  40.4 0.8 shard_map.112
  41.3 1.4 %all-to-all-done.right = bf16[32,4,1024]{2,1,0:T(4,128)(2,1)S(1)} async-done(((bf16[32,4,1024]{2,1,0:T(4,128)(2,1)}), bf16[32,4,1024]{2,1,0:T(4,128)(2,1)S(1)}, u32[]{:S(2)}, u32[]{:S(2)}) %all-to-all-start) | async-done | bytes 262176 | tf_op jit(solution)/shard_map/all_to_all | solution.py:149
  42.6 0.0 copy-done.1
  42.6 3.2 %shard_map.113 = (bf16[64,1024]{1,0:T(8,128)(2,1)S(1)}, f32[64,1024]{1,0:T(8,128)S(1)}, bf16[128,1024]{1,0:T(8,128)(2,1)S(1)}, bf16[512,1024]{1,0:T(8,128)(2,1)S...) custom-call(bf16[32,4,1024]{2,1,0:T(4,128)(2,1)S(1)} %all-to-all-done.right, ...), custom_call_target="tpu_custom_call" | custom-call | flops 400000000 | bytes 2000000 | tf_op jit(solution)/shard_map/pallas_call | solution.py:132
  45.8 4.2 %collective-permute-start = (bf16[64,1024]{1,0:T(8,128)(2,1)S(1)}, bf16[64,1024]{1,0:T(8,128)(2,1)S(1)}, u32[]{:S(2)}, u32[]{:S(2)}) collective-permute-start(bf16[64,1024]{1,0:T(8,128)(2,1)S(1)} %get-tuple-element.28), channel_id=1, source_target_pairs={{0,256},{16,272},{32,288},{48,304},{64,320},{80,336},{96,352},{112... | collective-permute-start | bytes 393224 | tf_op jit(solution)/shard_map/ppermute | solution.py:193
  50.1 1.3 %shard_map.115 = bf16[128,512]{1,0:T(8,128)(2,1)} custom-call(bf16[128,1024]{1,0:T(8,128)(2,1)S(1)} %get-tuple-element.25.right_all, bf16[512,1024]{1,0:T(8,128)(2,1)S(1)} %get-tuple-element.26.d_tiles), custom_call_target="tpu_custom_call" | custom-call | flops 400000000 | bytes 2000000 | tf_op jit(solution)/shard_map/pallas_call | solution.py:132
  51.4 3.5 %all-to-all-start.1 = ((bf16[16,8,512]{2,1,0:T(8,128)(2,1)}), bf16[16,8,512]{2,1,0:T(8,128)(2,1)S(1)}, u32[]{:S(2)}, u32[]{:S(2)}) async-start(bf16[16,8,512]{2,1,0:T(8,128)(2,1)} %bitcast.2), calls=%async_computation.1 | async-start | bytes 262144 | tf_op jit(solution)/shard_map/all_to_all | solution.py:153
  54.9 0.0 collective-permute-done.came
  54.9 0.7 shard_map.116
  55.6 6.0 %all-to-all-done.1 = bf16[16,8,512]{2,1,0:T(8,128)(2,1)S(1)} async-done(((bf16[16,8,512]{2,1,0:T(8,128)(2,1)}), bf16[16,8,512]{2,1,0:T(8,128)(2,1)S(1)}, u32[]{:S(2)}, u32[]{:S(2)}) %all-to-all-start.1) | async-done | bytes 131104 | tf_op jit(solution)/shard_map/all_to_all | solution.py:153
  61.6 12.1 %all-to-all-start.2 = ((bf16[16,4,1024]{2,1,0:T(4,128)(2,1)}), bf16[16,4,1024]{2,1,0:T(4,128)(2,1)S(1)}, u32[]{:S(2)}, u32[]{:S(2)}) async-start(bf16[16,4,1024]{2,1,0:T(4,128)(2,1)} %shard_map.116), calls=%async_computation.2 | async-start | bytes 262144 | tf_op jit(solution)/shard_map/all_to_all | solution.py:153
  73.7 1.4 %shard_map.114 = bf16[16,32,128]{2,1,0:T(8,128)(2,1)} custom-call(f32[512,128]{1,0:T(8,128)S(1)} %get-tuple-element.23.middle, bf16[512,512]{1,0:T(8,128)(2,1)S(1)} %get-tuple-element.24.hidden, bf16[512,128]{1,0:T(8,128)(2,1)S(1)} %copy-done.4), custom_call_target="tpu_custom_call" | custom-call | flops 400000000 | bytes 2000000 | tf_op jit(solution)/shard_map/pallas_call | solution.py:132
  75.1 0.6 multiply_convert_fusion.1
  75.7 12.2 %all-to-all-done.2 = bf16[16,4,1024]{2,1,0:T(4,128)(2,1)S(1)} async-done(((bf16[16,4,1024]{2,1,0:T(4,128)(2,1)}), bf16[16,4,1024]{2,1,0:T(4,128)(2,1)S(1)}, u32[]{:S(2)}, u32[]{:S(2)}) %all-to-all-start.2) | async-done | bytes 131104 | tf_op jit(solution)/shard_map/all_to_all | solution.py:153
  87.9 0.1 convert_reduce_fusion
  88.0 0.6 multiply_convert_fusion
  (11 shorter events, 0.0 us)
Async XLA Ops:
  2.1 18.0 %copy-start.7 = (bf16[8,512]{1,0:T(8,128)(2,1)S(1)}, bf16[8,512]{1,0:T(8,128)(2,1)}, u32[]{:S(2)}) copy-start(bf16[8,512]{1,0:T(8,128)(2,1)} %param.9) | copy-start | bytes 24580
  2.1 37.6 %copy-start.3 = (bf16[16,32,128]{2,1,0:T(8,128)(2,1)S(1)}, bf16[16,32,128]{2,1,0:T(8,128)(2,1)}, u32[]{:S(2)}) copy-start(bf16[16,32,128]{2,1,0:T(8,128)(2,1)} %pair_cot.1) | copy-start | bytes 393220
  2.1 37.6 %copy-start.4 = (bf16[512,128]{1,0:T(8,128)(2,1)S(1)}, bf16[512,128]{1,0:T(8,128)(2,1)}, u32[]{:S(2)}) copy-start(bf16[512,128]{1,0:T(8,128)(2,1)} %down.3) | copy-start | bytes 393220
  2.1 40.5 %all-to-all-start = ((bf16[32,4,1024]{2,1,0:T(4,128)(2,1)}), bf16[32,4,1024]{2,1,0:T(4,128)(2,1)S(1)}, u32[]{:S(2)}, u32[]{:S(2)}) async-start(bf16[32,4,1024]{2,1,0:T(4,128)(2,1)} %broadcast_in_dim.3), calls=%async_computation | async-start | bytes 524288 | tf_op jit(solution)/shard_map/all_to_all | solution.py:149
  20.1 19.7 %copy-start.2 = (bf16[16,32,128]{2,1,0:T(8,128)(2,1)S(1)}, bf16[16,32,128]{2,1,0:T(8,128)(2,1)}, u32[]{:S(2)}) copy-start(bf16[16,32,128]{2,1,0:T(8,128)(2,1)} %pair_in.1) | copy-start | bytes 393220
  39.7 0.7 copy-start.5
  39.7 0.7 copy-start.6
  40.4 2.2 %copy-start = (bf16[1024,128]{1,0:T(8,128)(2,1)S(1)}, bf16[1024,128]{1,0:T(8,128)(2,1)}, u32[]{:S(2)}) copy-start(bf16[1024,128]{1,0:T(8,128)(2,1)} %weight.1) | copy-start | bytes 786436
  40.4 2.2 %copy-start.1 = (bf16[128,512]{1,0:T(8,128)(2,1)S(1)}, bf16[128,512]{1,0:T(8,128)(2,1)}, u32[]{:S(2)}) copy-start(bf16[128,512]{1,0:T(8,128)(2,1)} %up.1) | copy-start | bytes 393220
  45.8 9.1 %collective-permute-start = (bf16[64,1024]{1,0:T(8,128)(2,1)S(1)}, bf16[64,1024]{1,0:T(8,128)(2,1)S(1)}, u32[]{:S(2)}, u32[]{:S(2)}) collective-permute-start(bf16[64,1024]{1,0:T(8,128)(2,1)S(1)} %get-tuple-element.28), channel_id=1, source_target_pairs={{0,256},{16,272},{32,288},{48,304},{64,320},{80,336},{96,352},{112... | collective-permute-start | bytes 393224 | tf_op jit(solution)/shard_map/ppermute | solution.py:193
  51.4 10.2 %all-to-all-start.1 = ((bf16[16,8,512]{2,1,0:T(8,128)(2,1)}), bf16[16,8,512]{2,1,0:T(8,128)(2,1)S(1)}, u32[]{:S(2)}, u32[]{:S(2)}) async-start(bf16[16,8,512]{2,1,0:T(8,128)(2,1)} %bitcast.2), calls=%async_computation.1 | async-start | bytes 262144 | tf_op jit(solution)/shard_map/all_to_all | solution.py:153
  61.6 26.3 %all-to-all-start.2 = ((bf16[16,4,1024]{2,1,0:T(4,128)(2,1)}), bf16[16,4,1024]{2,1,0:T(4,128)(2,1)S(1)}, u32[]{:S(2)}, u32[]{:S(2)}) async-start(bf16[16,4,1024]{2,1,0:T(4,128)(2,1)} %shard_map.116), calls=%async_computation.2 | async-start | bytes 262144 | tf_op jit(solution)/shard_map/all_to_all | solution.py:153

commit v3 on v1

--- a/solution.py
+++ b/solution.py
@@ -10,6 +10,7 @@
 GROUPS = 128 // C
 F32 = jnp.float32
 BF16 = jnp.bfloat16
+FIRST = 11
 NN = (((1,), (0,)), ((), ()))
 NT = (((1,), (1,)), ((), ()))
 TN = (((0,), (0,)), ((), ()))
@@ -64,19 +65,31 @@
     back[...] = mm(cot, down[...], NT).astype(BF16)
 
 
+def from_first(count):
+    return [(FIRST + k) % count for k in range(count)]
+
+
 def pair_step(
-    right, left_t, left_p, pair_p, cot_p, back, gain, weight, bias, up,
-    grad_right, right_all, d_tiles, middle_out, hidden_out,
-    tall, outer,
+    right, left_t, left_p, pair_p, cot_p, back, weight, up, gain_in, bias_in,
+    away, kept, middle_out, hidden_out, grad_left,
+    tall, outer, right_all, d_tiles, partial, gain, bias, sems,
 ):
+    fetch_gain = pltpu.make_async_copy(gain_in, gain, sems.at[0])
+    fetch_bias = pltpu.make_async_copy(bias_in, bias, sems.at[1])
+    fetch_gain.start()
+    fetch_bias.start()
     owners, each, width = right.shape
     rows = left_t.shape[0] // C
-    for k in range(owners):
-        tall[k * each : (k + 1) * each, :] = right[k].astype(F32)
+    for k, z in enumerate(from_first(owners // 2)):
+        for at, block in ((z, k), (z + owners // 2, k + owners // 2)):
+            tall[at * each : (at + 1) * each, :] = right[block].astype(F32)
     right_all[...] = tall[: owners * each, :].astype(BF16)
     tall[...] = mm(left_t[...], right_all[...])
     regroup(tall, outer, rows, 1.0 / SEQS)
-    middle = pair_p[...].astype(F32) + mm(outer[...], weight[...]) + bias[...]
+    update = mm(outer[...], weight[...])
+    fetch_gain.wait()
+    fetch_bias.wait()
+    middle = pair_p[...].astype(F32) + update + bias[...]
     middle_out[...] = middle
     centre = jnp.mean(middle, axis=-1, keepdims=True)
     centred = middle - centre
@@ -95,84 +108,125 @@
     )
     tall[...] = mm(d_middle.astype(BF16), weight[...], NT)
     regroup(tall, d_tiles, rows)
-    tall[: owners * each, :] = mm(left_p[...], d_tiles[...])
-    for k in range(owners):
-        grad_right[k] = tall[k * each : (k + 1) * each, :].astype(BF16)
-
-
-def finish(right_all, d_tiles, middle, hidden, down, grad_left, pair_out):
+    partial[...] = mm(right_all[...], d_tiles[...], NT).astype(BF16)
+    send = pltpu.make_async_copy(partial, grad_left, sems.at[2])
+    send.start()
+    half = SEQS // 2
+    mine = lax.axis_index("row") // (owners // 2)
+    away[...] = mm(left_p[pl.ds((1 - mine) * half, half), :], d_tiles[...]).astype(BF16)
+    kept[...] = mm(left_p[pl.ds(mine * half, half), :], d_tiles[...])
+    send.wait()
+
+
+def left_sum(arrived, grad_left):
+    total = jnp.sum(arrived[...].astype(F32), axis=0)
+    mine = (total * (1.0 / SEQS)).astype(BF16)
+    grad_left[...] = mm(mine, swap_rows(C, grad_left.shape[1] // C)).astype(BF16)
+
+
+def right_sum(arrived, grad_right):
+    total = jnp.sum(arrived[...].astype(F32), axis=0)
+    grad_right[...] = (total * (1.0 / SEQS)).astype(BF16)
+
+
+def join_halves(kept, came, tiles, total):
+    owners, each, _ = tiles.shape
+    total[...] = kept[...] + came[...].astype(F32)
+    for k, z in enumerate(from_first(owners)):
+        tiles[k] = total[z * each : (z + 1) * each, :].astype(BF16)
+
+
+def finish(middle, hidden, down, pair_out):
     rows, cols, _ = pair_out.shape
-    swap = swap_rows(C, rows)
-    swap_pair = swap if cols == C else swap_rows(cols, rows)
-    partial = mm(right_all[...], d_tiles[...], NT).astype(BF16)
-    grad_left[...] = mm(partial, swap).astype(BF16)
+    swap_pair = swap_rows(cols, rows)
     out = (middle[...] + mm(hidden[...], down[...])).astype(BF16)
     pair_out[...] = mm(swap_pair, out, TN).astype(BF16).reshape(pair_out.shape)
 
 
-def on_core(kernel, outs, scratch=()):
-    whole = pl.BlockSpec(memory_space=pltpu.VMEM)
-
-    def run(*args):
-        return pl.pallas_call(
-            kernel,
-            out_shape=[jax.ShapeDtypeStruct(*out) for out in outs],
-            in_specs=[whole] * len(args),
-            out_specs=[whole] * len(outs),
-            scratch_shapes=[pltpu.VMEM(*s) for s in scratch],
-            compiler_params=pltpu.CompilerParams(vmem_limit_bytes=32 << 20),
-            cost_estimate=pl.CostEstimate(
-                flops=400_000_000, bytes_accessed=2_000_000, transcendentals=0
-            ),
-        )(*args)
-
-    return run
-
-
-def sent_to_all(shard, axis):
-    copies = jnp.broadcast_to(shard, (lax.axis_size(axis), *shard.shape))
-    return lax.all_to_all(copies, axis, split_axis=0, concat_axis=0, tiled=True)
-
-
-def sum_at_owner(tiles, axis):
-    arrived = lax.all_to_all(tiles, axis, split_axis=0, concat_axis=0, tiled=True)
-    return (arrived.astype(F32).sum(axis=0) * (1.0 / SEQS)).astype(BF16)
+def in_hbm(x):
+    return pltpu.with_memory_space_constraint(x, pltpu.HBM)
+
+
+VMEM = pl.BlockSpec(memory_space=pltpu.VMEM)
+HBM = pl.BlockSpec(memory_space=pltpu.HBM)
+
+
+def on_core(kernel, args, outs, scratch=(), far_in=0, far_out=0):
+    return pl.pallas_call(
+        kernel,
+        out_shape=[jax.ShapeDtypeStruct(*out) for out in outs],
+        in_specs=[VMEM] * (len(args) - far_in) + [HBM] * far_in,
+        out_specs=[VMEM] * (len(outs) - far_out) + [HBM] * far_out,
+        scratch_shapes=[pltpu.VMEM(*s) if isinstance(s, tuple) else s for s in scratch],
+        compiler_params=pltpu.CompilerParams(vmem_limit_bytes=32 << 20),
+        cost_estimate=pl.CostEstimate(
+            flops=400_000_000, bytes_accessed=2_000_000, transcendentals=0
+        ),
+    )(*args)
+
+
+def to_each(tiles, axis, groups=None):
+    return lax.all_to_all(
+        tiles, axis, split_axis=0, concat_axis=0, tiled=True, axis_index_groups=groups
+    )
 
 
 def on_device(left, right, pair_in, pair_cot, ln_gain, out_weight, out_bias, trans_up, trans_down):
     rows, cols, dim = pair_in.shape
     cells, ffn = rows * cols, trans_up.shape[1]
-    right_blocks = sent_to_all(right, "row")
+    left_size, right_size = rows * C, cols * C
+    owners = lax.axis_size("row")
+    half = owners // 2
+    halves = [[start + z for z in from_first(half)] for start in (0, half)]
+    copies = jnp.broadcast_to(right, (owners, *right.shape))
+    right_blocks = to_each(copies, "row", [halves[0] + halves[1]])
     left_all = lax.all_gather(left, "col", axis=0, tiled=True)
     left_t, left_p, pair_p, cot_p, back = on_core(
         prepare,
-        [
-            ((rows * C, SEQS), BF16),
-            ((SEQS, rows * C), BF16),
+        [left_all, pair_in, pair_cot, trans_down],
+        [
+            ((left_size, SEQS), BF16),
+            ((SEQS, left_size), BF16),
             ((cells, dim), BF16),
             ((cells, dim), BF16),
             ((cells, ffn), BF16),
         ],
-    )(left_all, pair_in, pair_cot, trans_down)
-    grad_right, right_all, d_tiles, middle, hidden = on_core(
+    )
+    away, kept, middle, hidden, grad_left = on_core(
         pair_step,
         [
-            (right_blocks.shape, BF16),
-            ((SEQS, cols * C), BF16),
-            ((rows * C, cols * C), BF16),
+            right_blocks, left_t, left_p, pair_p, cot_p, back, out_weight, trans_up,
+            in_hbm(ln_gain.reshape(1, dim)), in_hbm(out_bias.reshape(1, dim)),
+        ],
+        [
+            ((SEQS // 2, right_size), BF16),
+            ((SEQS // 2, right_size), F32),
             ((cells, dim), F32),
             ((cells, ffn), BF16),
-        ],
-        [((max(rows * C, cells), cols * C), F32), ((cells, C * C), BF16)],
-    )(
-        right_blocks, left_t, left_p, pair_p, cot_p, back,
-        ln_gain.reshape(1, dim), out_weight, out_bias.reshape(1, dim), trans_up,
-    )
-    grad_right = sum_at_owner(grad_right, "row")
-    grad_left, pair_out = on_core(
-        finish, [((SEQS, rows * C), BF16), (pair_in.shape, BF16)]
-    )(right_all, d_tiles, middle, hidden, trans_down)
-    grad_left = sum_at_owner(grad_left.reshape(-1, *left.shape), "col")
+            ((SEQS, left_size), BF16),
+        ],
+        [
+            ((max(left_size, cells), max(right_size, C * C)), F32),
+            ((cells, C * C), BF16),
+            ((SEQS, right_size), BF16),
+            ((left_size, right_size), BF16),
+            ((SEQS, left_size), BF16),
+            ((1, dim), F32),
+            ((1, dim), F32),
+            pltpu.SemaphoreType.DMA((3,)),
+        ],
+        far_in=2,
+        far_out=1,
+    )
+    came = lax.ppermute(away, "row", [(k, (k + half) % owners) for k in range(owners)])
+    left_tiles = to_each(grad_left.reshape(-1, *left.shape), "col")
+    (tiles,) = on_core(
+        join_halves, [kept, came], [((half, *right.shape), BF16)], [((SEQS // 2, right_size), F32)]
+    )
+    right_tiles = to_each(tiles, "row", halves)
+    (pair_out,) = on_core(finish, [middle, hidden, trans_down], [(pair_in.shape, BF16)])
+    (grad_left,) = on_core(left_sum, [left_tiles], [(left.shape, BF16)])
+    (grad_right,) = on_core(right_sum, [right_tiles], [(right.shape, BF16)])
     return pair_out, grad_left, grad_right
 
 

time: 95.8 us -> 83.5 us (0.87)
  blocking collectives: 34.1 us -> 21 us
  starting transfers between devices: 28.6 us -> 39.3 us
  waiting for transfers between devices: 21 us -> 11.8 us
  Pallas kernels: 6.95 us -> 8.56 us
  other arithmetic: 1.36 us -> 0 us
    all_to_all x1 -> x0, blocking collectives: 13.6 us -> none  [sum_at_owner(): lax.all_to_all(tiles, axis, split_axis=0, concat_axis=0, tiled=True)]
    all_to_all x2 -> x3, waiting for transfers between devices: 21 us -> 11.8 us  [to_each(): lax.all_to_all(tiles, axis, split_axis=0, concat_axis=0, tiled=True, axis...]
    all_to_all x2 -> x3, starting transfers between devices: 28.6 us -> 34.4 us  [to_each(): lax.all_to_all(tiles, axis, split_axis=0, concat_axis=0, tiled=True, axis...]
    ppermute x0 -> x1, starting transfers between devices: none -> 4.92 us  [on_device(): lax.ppermute(away, 'row', [(k, (k + half) % owners) for k in range(owners)])]
    pallas_call x3 -> x6, Pallas kernels: 6.95 us -> 8.56 us  [on_core(): pl.pallas_call(kernel, out_shape=[jax.ShapeDtypeStruct(*out) for out in o...]
    convert_element_type x2 -> x0, other arithmetic: 1.21 us -> none  [sum_at_owner(): return (arrived.astype(F32).sum(axis=0) * (1.0 / SEQS)).astype(BF16)]
  transfers between devices with their start and end apart: 2 -> 4, of which waited for: 2 -> 2; matrix products, arithmetic and copies ran while one was open for 1% -> 0% of each run, Pallas kernels for 1% -> 5%
where the time goes in v3:
time: 83.5 us; the launch traced here: 83 us
  starting transfers between devices  39.3 us (47%)
  blocking collectives  21 us (25%)
  waiting for transfers between devices  11.8 us (14%)
  Pallas kernels  8.56 us (10%)
  local copies, waits for them, and re-layouts  1.59 us (2%)
    all_to_all x3, starting transfers between devices, to_each(): lax.all_to_all(tiles, axis, split_axis=0, concat_axis=0, tiled=True, axis...  34.4 us
    all_gather x1, blocking collectives, on_device(): left_all = lax.all_gather(left, 'col', axis=0, tiled=True)  21 us
    all_to_all x3, waiting for transfers between devices, to_each(): lax.all_to_all(tiles, axis, split_axis=0, concat_axis=0, tiled=True, axis...  11.8 us
    pallas_call x6, Pallas kernels, on_core(): pl.pallas_call(kernel, out_shape=[jax.ShapeDtypeStruct(*out) for out in o...  8.56 us
    ppermute x1, starting transfers between devices, on_device(): lax.ppermute(away, 'row', [(k, (k + half) % owners) for k in range(owners)])  4.92 us
  transfers between devices with their start and end apart: 4, of which 2 were waited for; matrix products, arithmetic and copies ran while one was open for 0% of the time, Pallas kernels for 5%

profile of v3, /device:TPU:1, one launch (start us, length us, event | category | flops | bytes accessed | tf_op | source)
XLA Modules:
  0.0 83.0 jit_solution(14889726651288797736)
XLA Ops:
  0.6 1.5 %broadcast_in_dim.3 = bf16[32,4,1024]{2,1,0:T(4,128)(2,1)} broadcast(bf16[4,1024]{1,0:T(4,128)(2,1)} %param.10), dimensions={1,2} | broadcast | bytes 270336 | tf_op jit(solution)/shard_map/broadcast_in_dim | solution.py:181
  2.1 19.2 %all-to-all-start = ((bf16[32,4,1024]{2,1,0:T(4,128)(2,1)}), bf16[32,4,1024]{2,1,0:T(4,128)(2,1)S(1)}, u32[]{:S(2)}, u32[]{:S(2)}) async-start(bf16[32,4,1024]{2,1,0:T(4,128)(2,1)} %broadcast_in_dim.3), calls=%async_computation | async-start | bytes 524288 | tf_op jit(solution)/shard_map/all_to_all | solution.py:169
  21.3 0.0 copy-done.5
  21.3 0.0 copy-start.2
  21.3 21.0 %all_gather.3.left = bf16[128,512]{1,0:T(8,128)(2,1)S(1)} all-gather(bf16[8,512]{1,0:T(8,128)(2,1)S(1)} %copy-done.5), channel_id=1, replica_groups=mesh['row'=32,'col'=16] {'col'}, dimensions={0}, use_global_device_ids=true | all-gather | bytes 139264 | tf_op jit(solution)/shard_map/all_gather | solution.py:183
  42.3 0.0 copy-done.3
  42.3 0.0 copy-done.4
  42.3 0.0 copy-start
  42.3 0.0 copy-start.1
  42.3 0.9 %shard_map.112 = (bf16[512,128]{1,0:T(8,128)(2,1)S(1)}, bf16[128,512]{1,0:T(8,128)(2,1)S(1)}, bf16[512,128]{1,0:T(8,128)(2,1)S(1)}, bf16[512,128]{1,0:T(8,128)(2,1)S(1)}, bf16[512,512]{1,0:T(8,128)(2,1)S(1)}) custom-call(bf16[128,512]{1,0:T(8,128)(2,1)S(1)} %all_gather.3.left, bf16[16,32,128]{2,1,0:T(8,128)(2,1)S(1)} %copy-done.2, ...), custom_call_target="tpu_custom_call" | custom-call | flops 400000000 | bytes 2000000 | tf_op jit(solution)/shard_map/pallas_call | solution.py:155
  43.2 0.0 all-to-all-done.right
  43.2 0.1 copy-done
  43.3 0.0 copy-done.1
  43.3 4.1 %shard_map.113 = (bf16[64,1024]{1,0:T(8,128)(2,1)S(1)}, f32[64,1024]{1,0:T(8,128)S(1)}, f32[512,128]{1,0:T(8,128)S(1)}, bf16[512,512]{1,0:T(8,128)(2,1)S(1)}, bf16[128,512]{1,0:T(8,128)(2,1)}) custom-call(bf16[32,4,1024]{2,1,0:T(4,128)(2,1)S(1)} %all-to-all-done.right, bf16[512,128]{1,0:T(8,128)(2,1)S(1)} %get-tuple-element.13.left_t, ...), custom_call_target="tpu_custom_call" | custom-call | flops 400000000 | bytes 2000000 | tf_op jit(solution)/shard_map/pallas_call | solution.py:155
  47.4 4.9 %collective-permute-start = (bf16[64,1024]{1,0:T(8,128)(2,1)S(1)}, bf16[64,1024]{1,0:T(8,128)(2,1)S(1)}, u32[]{:S(2)}, u32[]{:S(2)}) collective-permute-start(bf16[64,1024]{1,0:T(8,128)(2,1)S(1)} %get-tuple-element.22), channel_id=1, source_target_pairs={{0,256},{16,272},{32,288},{48,304},{64,320},{80,336},{96,352},{112... | collective-permute-start | bytes 393224 | tf_op jit(solution)/shard_map/ppermute | solution.py:221
  52.3 3.8 %all-to-all-start.1 = ((bf16[16,8,512]{2,1,0:T(8,128)(2,1)}), bf16[16,8,512]{2,1,0:T(8,128)(2,1)S(1)}, u32[]{:S(2)}, u32[]{:S(2)}) async-start(bf16[16,8,512]{2,1,0:T(8,128)(2,1)} %bitcast.2), calls=%async_computation.1 | async-start | bytes 262144 | tf_op jit(solution)/shard_map/all_to_all | solution.py:169
  56.1 0.0 collective-permute-done.came
  56.1 0.7 shard_map.116
  56.8 5.5 %all-to-all-done.1.arrived = bf16[16,8,512]{2,1,0:T(8,128)(2,1)S(1)} async-done(((bf16[16,8,512]{2,1,0:T(8,128)(2,1)}), bf16[16,8,512]{2,1,0:T(8,128)(2,1)S(1)}, u32[]{:S(2)}, u32[]{:S(2)}) %all-to-all-start.1) | async-done | bytes 131104 | tf_op jit(solution)/shard_map/all_to_all | solution.py:169
  62.3 11.5 %all-to-all-start.2 = ((bf16[16,4,1024]{2,1,0:T(4,128)(2,1)}), bf16[16,4,1024]{2,1,0:T(4,128)(2,1)S(1)}, u32[]{:S(2)}, u32[]{:S(2)}) async-start(bf16[16,4,1024]{2,1,0:T(4,128)(2,1)} %shard_map.116), calls=%async_computation.2 | async-start | bytes 262144 | tf_op jit(solution)/shard_map/all_to_all | solution.py:169
  73.8 1.4 %shard_map.114 = bf16[16,32,128]{2,1,0:T(8,128)(2,1)} custom-call(f32[512,128]{1,0:T(8,128)S(1)} %get-tuple-element.18.middle, bf16[512,512]{1,0:T(8,128)(2,1)S(1)} %get-tuple-element.19.hidden, bf16[512,128]{1,0:T(8,128)(2,1)S(1)} %copy-done.4), custom_call_target="tpu_custom_call" | custom-call | flops 400000000 | bytes 2000000 | tf_op jit(solution)/shard_map/pallas_call | solution.py:155
  75.2 0.8 %shard_map.115 = bf16[8,512]{1,0:T(8,128)(2,1)} custom-call(bf16[16,8,512]{2,1,0:T(8,128)(2,1)S(1)} %all-to-all-done.1.arrived), custom_call_target="tpu_custom_call" | custom-call | flops 400000000 | bytes 2000000 | tf_op jit(solution)/shard_map/pallas_call | solution.py:155
  76.1 6.3 %all-to-all-done.2.arrived = bf16[16,4,1024]{2,1,0:T(4,128)(2,1)S(1)} async-done(((bf16[16,4,1024]{2,1,0:T(4,128)(2,1)}), bf16[16,4,1024]{2,1,0:T(4,128)(2,1)S(1)}, u32[]{:S(2)}, u32[]{:S(2)}) %all-to-all-start.2) | async-done | bytes 131104 | tf_op jit(solution)/shard_map/all_to_all | solution.py:169
  82.4 0.7 shard_map.117
  (4 shorter events, 0.0 us)
Async XLA Ops:
  2.1 19.2 %copy-start.5 = (bf16[8,512]{1,0:T(8,128)(2,1)S(1)}, bf16[8,512]{1,0:T(8,128)(2,1)}, u32[]{:S(2)}) copy-start(bf16[8,512]{1,0:T(8,128)(2,1)} %param.9) | copy-start | bytes 24580
  2.1 40.2 %copy-start.3 = (bf16[16,32,128]{2,1,0:T(8,128)(2,1)S(1)}, bf16[16,32,128]{2,1,0:T(8,128)(2,1)}, u32[]{:S(2)}) copy-start(bf16[16,32,128]{2,1,0:T(8,128)(2,1)} %pair_cot.1) | copy-start | bytes 393220
  2.1 40.2 %copy-start.4 = (bf16[512,128]{1,0:T(8,128)(2,1)S(1)}, bf16[512,128]{1,0:T(8,128)(2,1)}, u32[]{:S(2)}) copy-start(bf16[512,128]{1,0:T(8,128)(2,1)} %down.3) | copy-start | bytes 393220
  2.1 41.1 %all-to-all-start = ((bf16[32,4,1024]{2,1,0:T(4,128)(2,1)}), bf16[32,4,1024]{2,1,0:T(4,128)(2,1)S(1)}, u32[]{:S(2)}, u32[]{:S(2)}) async-start(bf16[32,4,1024]{2,1,0:T(4,128)(2,1)} %broadcast_in_dim.3), calls=%async_computation | async-start | bytes 524288 | tf_op jit(solution)/shard_map/all_to_all | solution.py:169
  21.3 21.0 %copy-start.2 = (bf16[16,32,128]{2,1,0:T(8,128)(2,1)S(1)}, bf16[16,32,128]{2,1,0:T(8,128)(2,1)}, u32[]{:S(2)}) copy-start(bf16[16,32,128]{2,1,0:T(8,128)(2,1)} %pair_in.1) | copy-start | bytes 393220
  42.3 1.0 %copy-start = (bf16[1024,128]{1,0:T(8,128)(2,1)S(1)}, bf16[1024,128]{1,0:T(8,128)(2,1)}, u32[]{:S(2)}) copy-start(bf16[1024,128]{1,0:T(8,128)(2,1)} %weight.1) | copy-start | bytes 786436
  42.3 1.0 %copy-start.1 = (bf16[128,512]{1,0:T(8,128)(2,1)S(1)}, bf16[128,512]{1,0:T(8,128)(2,1)}, u32[]{:S(2)}) copy-start(bf16[128,512]{1,0:T(8,128)(2,1)} %up.1) | copy-start | bytes 393220
  47.4 8.7 %collective-permute-start = (bf16[64,1024]{1,0:T(8,128)(2,1)S(1)}, bf16[64,1024]{1,0:T(8,128)(2,1)S(1)}, u32[]{:S(2)}, u32[]{:S(2)}) collective-permute-start(bf16[64,1024]{1,0:T(8,128)(2,1)S(1)} %get-tuple-element.22), channel_id=1, source_target_pairs={{0,256},{16,272},{32,288},{48,304},{64,320},{80,336},{96,352},{112... | collective-permute-start | bytes 393224 | tf_op jit(solution)/shard_map/ppermute | solution.py:221
  52.3 10.0 %all-to-all-start.1 = ((bf16[16,8,512]{2,1,0:T(8,128)(2,1)}), bf16[16,8,512]{2,1,0:T(8,128)(2,1)S(1)}, u32[]{:S(2)}, u32[]{:S(2)}) async-start(bf16[16,8,512]{2,1,0:T(8,128)(2,1)} %bitcast.2), calls=%async_computation.1 | async-start | bytes 262144 | tf_op jit(solution)/shard_map/all_to_all | solution.py:169
  62.3 20.1 %all-to-all-start.2 = ((bf16[16,4,1024]{2,1,0:T(4,128)(2,1)}), bf16[16,4,1024]{2,1,0:T(4,128)(2,1)S(1)}, u32[]{:S(2)}, u32[]{:S(2)}) async-start(bf16[16,4,1024]{2,1,0:T(4,128)(2,1)} %shard_map.116), calls=%async_computation.2 | async-start | bytes 262144 | tf_op jit(solution)/shard_map/all_to_all | solution.py:169

commit v4 on v3

--- a/solution.py
+++ b/solution.py
@@ -10,6 +10,7 @@
 GROUPS = 128 // C
 F32 = jnp.float32
 BF16 = jnp.bfloat16
+Y, X, CORES = 4, 2, 2
 FIRST = 11
 NN = (((1,), (0,)), ((), ()))
 NT = (((1,), (1,)), ((), ()))
@@ -57,12 +58,22 @@
     rows, cols, _ = pair_in.shape
     swap = swap_rows(C, rows)
     swap_pair = swap if cols == C else swap_rows(cols, rows)
-    left_t[...] = mm(swap, left[...], NT).astype(BF16)
-    left_p[...] = mm(left[...], swap, NT).astype(BF16)
+    ring = chip_ring()
+    each = left.shape[0] // len(ring)
+    came = left[...].astype(F32)
+    blocks = [came[ring.index(k) * each : (ring.index(k) + 1) * each] for k in range(len(ring))]
+    left_all = jnp.concatenate(blocks, axis=0).astype(BF16)
+    left_t[...] = mm(swap, left_all, NT).astype(BF16)
+    left_p[...] = mm(left_all, swap, NT).astype(BF16)
     pair_p[...] = mm(swap_pair, pair_in[...].reshape(rows * cols, -1)).astype(BF16)
     cot = mm(swap_pair, pair_cot[...].reshape(rows * cols, -1)).astype(BF16)
     cot_p[...] = cot
     back[...] = mm(cot, down[...], NT).astype(BF16)
+
+
+def chip_ring():
+    chips = [(y, 0) for y in range(Y)] + [(y, 1) for y in reversed(range(Y))]
+    return [(y * X + x) * CORES + core for y, x in chips for core in range(CORES)]
 
 
 def from_first(count):
@@ -180,10 +191,12 @@
     halves = [[start + z for z in from_first(half)] for start in (0, half)]
     copies = jnp.broadcast_to(right, (owners, *right.shape))
     right_blocks = to_each(copies, "row", [halves[0] + halves[1]])
-    left_all = lax.all_gather(left, "col", axis=0, tiled=True)
+    left_blocks = lax.all_gather(
+        left, "col", axis=0, tiled=True, axis_index_groups=[chip_ring()]
+    )
     left_t, left_p, pair_p, cot_p, back = on_core(
         prepare,
-        [left_all, pair_in, pair_cot, trans_down],
+        [left_blocks, pair_in, pair_cot, trans_down],
         [
             ((left_size, SEQS), BF16),
             ((SEQS, left_size), BF16),

time: 83.5 us -> 77.9 us (0.933)
  blocking collectives: 21 us -> 15.7 us
    all_gather x1, blocking collectives: 21 us -> 15.7 us  [on_device(): lax.all_gather(left, 'col', axis=0, tiled=True, axis_index_groups=[chip_r...]
where the time goes in v4:
time: 77.9 us; the launch traced here: 77.4 us
  starting transfers between devices  39.1 us (50%)
  blocking collectives  15.7 us (20%)
  waiting for transfers between devices  11.8 us (15%)
  Pallas kernels  8.56 us (11%)
  local copies, waits for them, and re-layouts  1.59 us (2%)
    all_to_all x3, starting transfers between devices, to_each(): lax.all_to_all(tiles, axis, split_axis=0, concat_axis=0, tiled=True, axis...  34.5 us
    all_gather x1, blocking collectives, on_device(): lax.all_gather(left, 'col', axis=0, tiled=True, axis_index_groups=[chip_r...  15.7 us
    all_to_all x3, waiting for transfers between devices, to_each(): lax.all_to_all(tiles, axis, split_axis=0, concat_axis=0, tiled=True, axis...  11.8 us
    pallas_call x6, Pallas kernels, on_core(): pl.pallas_call(kernel, out_shape=[jax.ShapeDtypeStruct(*out) for out in o...  8.56 us
    ppermute x1, starting transfers between devices, on_device(): lax.ppermute(away, 'row', [(k, (k + half) % owners) for k in range(owners)])  4.55 us
  transfers between devices with their start and end apart: 4, of which 2 were waited for; matrix products, arithmetic and copies ran while one was open for 0% of the time, Pallas kernels for 5%

profile of v4, /device:TPU:1, one launch (start us, length us, event | category | flops | bytes accessed | tf_op | source)
XLA Modules:
  0.0 77.4 jit_solution(8382018504239822819)
XLA Ops:
  0.6 1.5 %broadcast_in_dim.3 = bf16[32,4,1024]{2,1,0:T(4,128)(2,1)} broadcast(bf16[4,1024]{1,0:T(4,128)(2,1)} %param.10), dimensions={1,2} | broadcast | bytes 270336 | tf_op jit(solution)/shard_map/broadcast_in_dim | solution.py:192
  2.1 19.2 %all-to-all-start = ((bf16[32,4,1024]{2,1,0:T(4,128)(2,1)}), bf16[32,4,1024]{2,1,0:T(4,128)(2,1)S(1)}, u32[]{:S(2)}, u32[]{:S(2)}) async-start(bf16[32,4,1024]{2,1,0:T(4,128)(2,1)} %broadcast_in_dim.3), calls=%async_computation | async-start | bytes 524288 | tf_op jit(solution)/shard_map/all_to_all | solution.py:180
  21.3 0.0 copy-done.5
  21.3 0.0 copy-start.2
  21.3 15.7 %all_gather.3.left = bf16[128,512]{1,0:T(8,128)(2,1)S(1)} all-gather(bf16[8,512]{1,0:T(8,128)(2,1)S(1)} %copy-done.5), channel_id=1, replica_groups={{0,1,4,5,8,9,12,13,14,15,10,11,6,7,2,3},{16,17,20,21,24,25,28,29,30,31,..., dimensions={0}, use_global_device_ids=true | all-gather | bytes 139264 | tf_op jit(solution)/shard_map/all_gather | solution.py:194
  37.0 0.0 copy-done.3
  37.0 0.0 copy-done.2
  37.0 0.0 copy-start
  37.1 0.0 copy-start.1
  37.1 0.8 %shard_map.112 = (bf16[512,128]{1,0:T(8,128)(2,1)S(1)}, bf16[128,512]{1,0:T(8,128)(2,1)S(1)}, bf16[512,128]{1,0:T(8,128)(2,1)S(1)}, bf16[512,128]{1,0:T(8,128)(2,1)S(1)}, bf16[512,512]{1,0:T(8,128)(2,1)S(1)}) custom-call(bf16[128,512]{1,0:T(8,128)(2,1)S(1)} %all_gather.3.left, bf16[16,32,128]{2,1,0:T(8,128)(2,1)S(1)} %copy-done.2, ...), custom_call_target="tpu_custom_call" | custom-call | flops 400000000 | bytes 2000000 | tf_op jit(solution)/shard_map/pallas_call | solution.py:166
  37.9 0.0 all-to-all-done.right
  37.9 0.1 copy-done
  38.0 0.0 copy-done.1
  38.0 4.1 %shard_map.113 = (bf16[64,1024]{1,0:T(8,128)(2,1)S(1)}, f32[64,1024]{1,0:T(8,128)S(1)}, f32[512,128]{1,0:T(8,128)S(1)}, bf16[512,512]{1,0:T(8,128)(2,1)S(1)}, bf16[128,512]{1,0:T(8,128)(2,1)}) custom-call(bf16[32,4,1024]{2,1,0:T(4,128)(2,1)S(1)} %all-to-all-done.right, bf16[512,128]{1,0:T(8,128)(2,1)S(1)} %get-tuple-element.13.left_t, ...), custom_call_target="tpu_custom_call" | custom-call | flops 400000000 | bytes 2000000 | tf_op jit(solution)/shard_map/pallas_call | solution.py:166
  42.1 4.5 %collective-permute-start = (bf16[64,1024]{1,0:T(8,128)(2,1)S(1)}, bf16[64,1024]{1,0:T(8,128)(2,1)S(1)}, u32[]{:S(2)}, u32[]{:S(2)}) collective-permute-start(bf16[64,1024]{1,0:T(8,128)(2,1)S(1)} %get-tuple-element.22), channel_id=1, source_target_pairs={{0,256},{16,272},{32,288},{48,304},{64,320},{80,336},{96,352},{112... | collective-permute-start | bytes 393224 | tf_op jit(solution)/shard_map/ppermute | solution.py:234
  46.7 4.0 %all-to-all-start.1 = ((bf16[16,8,512]{2,1,0:T(8,128)(2,1)}), bf16[16,8,512]{2,1,0:T(8,128)(2,1)S(1)}, u32[]{:S(2)}, u32[]{:S(2)}) async-start(bf16[16,8,512]{2,1,0:T(8,128)(2,1)} %bitcast.2), calls=%async_computation.1 | async-start | bytes 262144 | tf_op jit(solution)/shard_map/all_to_all | solution.py:180
  50.7 0.0 collective-permute-done.came
  50.7 0.7 shard_map.116
  51.4 5.4 %all-to-all-done.1.arrived = bf16[16,8,512]{2,1,0:T(8,128)(2,1)S(1)} async-done(((bf16[16,8,512]{2,1,0:T(8,128)(2,1)}), bf16[16,8,512]{2,1,0:T(8,128)(2,1)S(1)}, u32[]{:S(2)}, u32[]{:S(2)}) %all-to-all-start.1) | async-done | bytes 131104 | tf_op jit(solution)/shard_map/all_to_all | solution.py:180
  56.9 11.3 %all-to-all-start.2 = ((bf16[16,4,1024]{2,1,0:T(4,128)(2,1)}), bf16[16,4,1024]{2,1,0:T(4,128)(2,1)S(1)}, u32[]{:S(2)}, u32[]{:S(2)}) async-start(bf16[16,4,1024]{2,1,0:T(4,128)(2,1)} %shard_map.116), calls=%async_computation.2 | async-start | bytes 262144 | tf_op jit(solution)/shard_map/all_to_all | solution.py:180
  68.2 1.4 %shard_map.114 = bf16[16,32,128]{2,1,0:T(8,128)(2,1)} custom-call(f32[512,128]{1,0:T(8,128)S(1)} %get-tuple-element.18.middle, bf16[512,512]{1,0:T(8,128)(2,1)S(1)} %get-tuple-element.19.hidden, bf16[512,128]{1,0:T(8,128)(2,1)S(1)} %copy-done.4), custom_call_target="tpu_custom_call" | custom-call | flops 400000000 | bytes 2000000 | tf_op jit(solution)/shard_map/pallas_call | solution.py:166
  69.6 0.8 %shard_map.115 = bf16[8,512]{1,0:T(8,128)(2,1)} custom-call(bf16[16,8,512]{2,1,0:T(8,128)(2,1)S(1)} %all-to-all-done.1.arrived), custom_call_target="tpu_custom_call" | custom-call | flops 400000000 | bytes 2000000 | tf_op jit(solution)/shard_map/pallas_call | solution.py:166
  70.5 6.3 %all-to-all-done.2.arrived = bf16[16,4,1024]{2,1,0:T(4,128)(2,1)S(1)} async-done(((bf16[16,4,1024]{2,1,0:T(4,128)(2,1)}), bf16[16,4,1024]{2,1,0:T(4,128)(2,1)S(1)}, u32[]{:S(2)}, u32[]{:S(2)}) %all-to-all-start.2) | async-done | bytes 131104 | tf_op jit(solution)/shard_map/all_to_all | solution.py:180
  76.8 0.7 shard_map.117
  (4 shorter events, 0.0 us)
Async XLA Ops:
  2.1 19.2 %copy-start.5 = (bf16[8,512]{1,0:T(8,128)(2,1)S(1)}, bf16[8,512]{1,0:T(8,128)(2,1)}, u32[]{:S(2)}) copy-start(bf16[8,512]{1,0:T(8,128)(2,1)} %param.9) | copy-start | bytes 24580
  2.1 34.9 %copy-start.3 = (bf16[16,32,128]{2,1,0:T(8,128)(2,1)S(1)}, bf16[16,32,128]{2,1,0:T(8,128)(2,1)}, u32[]{:S(2)}) copy-start(bf16[16,32,128]{2,1,0:T(8,128)(2,1)} %pair_cot.1) | copy-start | bytes 393220
  2.1 34.9 %copy-start.4 = (bf16[512,128]{1,0:T(8,128)(2,1)S(1)}, bf16[512,128]{1,0:T(8,128)(2,1)}, u32[]{:S(2)}) copy-start(bf16[512,128]{1,0:T(8,128)(2,1)} %down.3) | copy-start | bytes 393220
  2.1 35.8 %all-to-all-start = ((bf16[32,4,1024]{2,1,0:T(4,128)(2,1)}), bf16[32,4,1024]{2,1,0:T(4,128)(2,1)S(1)}, u32[]{:S(2)}, u32[]{:S(2)}) async-start(bf16[32,4,1024]{2,1,0:T(4,128)(2,1)} %broadcast_in_dim.3), calls=%async_computation | async-start | bytes 524288 | tf_op jit(solution)/shard_map/all_to_all | solution.py:180
  21.3 15.8 %copy-start.2 = (bf16[16,32,128]{2,1,0:T(8,128)(2,1)S(1)}, bf16[16,32,128]{2,1,0:T(8,128)(2,1)}, u32[]{:S(2)}) copy-start(bf16[16,32,128]{2,1,0:T(8,128)(2,1)} %pair_in.1) | copy-start | bytes 393220
  37.0 1.0 %copy-start = (bf16[1024,128]{1,0:T(8,128)(2,1)S(1)}, bf16[1024,128]{1,0:T(8,128)(2,1)}, u32[]{:S(2)}) copy-start(bf16[1024,128]{1,0:T(8,128)(2,1)} %weight.1) | copy-start | bytes 786436
  37.1 1.0 %copy-start.1 = (bf16[128,512]{1,0:T(8,128)(2,1)S(1)}, bf16[128,512]{1,0:T(8,128)(2,1)}, u32[]{:S(2)}) copy-start(bf16[128,512]{1,0:T(8,128)(2,1)} %up.1) | copy-start | bytes 393220
  42.1 8.6 %collective-permute-start = (bf16[64,1024]{1,0:T(8,128)(2,1)S(1)}, bf16[64,1024]{1,0:T(8,128)(2,1)S(1)}, u32[]{:S(2)}, u32[]{:S(2)}) collective-permute-start(bf16[64,1024]{1,0:T(8,128)(2,1)S(1)} %get-tuple-element.22), channel_id=1, source_target_pairs={{0,256},{16,272},{32,288},{48,304},{64,320},{80,336},{96,352},{112... | collective-permute-start | bytes 393224 | tf_op jit(solution)/shard_map/ppermute | solution.py:234
  46.7 10.2 %all-to-all-start.1 = ((bf16[16,8,512]{2,1,0:T(8,128)(2,1)}), bf16[16,8,512]{2,1,0:T(8,128)(2,1)S(1)}, u32[]{:S(2)}, u32[]{:S(2)}) async-start(bf16[16,8,512]{2,1,0:T(8,128)(2,1)} %bitcast.2), calls=%async_computation.1 | async-start | bytes 262144 | tf_op jit(solution)/shard_map/all_to_all | solution.py:180
  56.9 19.9 %all-to-all-start.2 = ((bf16[16,4,1024]{2,1,0:T(4,128)(2,1)}), bf16[16,4,1024]{2,1,0:T(4,128)(2,1)S(1)}, u32[]{:S(2)}, u32[]{:S(2)}) async-start(bf16[16,4,1024]{2,1,0:T(4,128)(2,1)} %shard_map.116), calls=%async_computation.2 | async-start | bytes 262144 | tf_op jit(solution)/shard_map/all_to_all | solution.py:180

commit v5 on v4

--- a/solution.py
+++ b/solution.py
@@ -11,7 +11,7 @@
 F32 = jnp.float32
 BF16 = jnp.bfloat16
 Y, X, CORES = 4, 2, 2
-FIRST = 11
+OUT, BACK = (11, 1), (8, 7)
 NN = (((1,), (0,)), ((), ()))
 NT = (((1,), (1,)), ((), ()))
 TN = (((0,), (0,)), ((), ()))
@@ -49,9 +49,10 @@
             ]
             if scale is not None:
                 tiles = [tile * scale for tile in tiles]
+            tiles = [tile.astype(BF16) for tile in tiles]
             for t, tile in enumerate(exchange(tiles)):
                 at = (GROUPS * h + t) * rows
-                dst[at : at + rows, g * 128 : (g + 1) * 128] = tile.astype(dst.dtype)
+                dst[at : at + rows, g * 128 : (g + 1) * 128] = tile
 
 
 def prepare(left, pair_in, pair_cot, down, left_t, left_p, pair_p, cot_p, back):
@@ -76,8 +77,9 @@
     return [(y * X + x) * CORES + core for y, x in chips for core in range(CORES)]
 
 
-def from_first(count):
-    return [(FIRST + k) % count for k in range(count)]
+def listed(count, order):
+    first, stride = order
+    return [(first + stride * k) % count for k in range(count)]
 
 
 def pair_step(
@@ -91,7 +93,7 @@
     fetch_bias.start()
     owners, each, width = right.shape
     rows = left_t.shape[0] // C
-    for k, z in enumerate(from_first(owners // 2)):
+    for k, z in enumerate(listed(owners // 2, OUT)):
         for at, block in ((z, k), (z + owners // 2, k + owners // 2)):
             tall[at * each : (at + 1) * each, :] = right[block].astype(F32)
     right_all[...] = tall[: owners * each, :].astype(BF16)
@@ -143,7 +145,7 @@
 def join_halves(kept, came, tiles, total):
     owners, each, _ = tiles.shape
     total[...] = kept[...] + came[...].astype(F32)
-    for k, z in enumerate(from_first(owners)):
+    for k, z in enumerate(listed(owners, BACK)):
         tiles[k] = total[z * each : (z + 1) * each, :].astype(BF16)
 
 
@@ -188,9 +190,11 @@
     left_size, right_size = rows * C, cols * C
     owners = lax.axis_size("row")
     half = owners // 2
-    halves = [[start + z for z in from_first(half)] for start in (0, half)]
+    out_order, back_order = (
+        [[start + z for z in listed(half, order)] for start in (0, half)] for order in (OUT, BACK)
+    )
     copies = jnp.broadcast_to(right, (owners, *right.shape))
-    right_blocks = to_each(copies, "row", [halves[0] + halves[1]])
+    right_blocks = to_each(copies, "row", [out_order[0] + out_order[1]])
     left_blocks = lax.all_gather(
         left, "col", axis=0, tiled=True, axis_index_groups=[chip_ring()]
     )
@@ -236,7 +240,7 @@
     (tiles,) = on_core(
         join_halves, [kept, came], [((half, *right.shape), BF16)], [((SEQS // 2, right_size), F32)]
     )
-    right_tiles = to_each(tiles, "row", halves)
+    right_tiles = to_each(tiles, "row", back_order)
     (pair_out,) = on_core(finish, [middle, hidden, trans_down], [(pair_in.shape, BF16)])
     (grad_left,) = on_core(left_sum, [left_tiles], [(left.shape, BF16)])
     (grad_right,) = on_core(right_sum, [right_tiles], [(right.shape, BF16)])

time: 77.9 us -> 76 us (0.976)
  waiting for transfers between devices: 11.8 us -> 9.47 us
    all_to_all x3, waiting for transfers between devices: 11.8 us -> 9.46 us  [to_each(): lax.all_to_all(tiles, axis, split_axis=0, concat_axis=0, tiled=True, axis...]
where the time goes in v5:
time: 76 us; the launch traced here: 74.9 us
  starting transfers between devices  39.2 us (52%)
  blocking collectives  15.7 us (21%)
  waiting for transfers between devices  9.47 us (12%)
  Pallas kernels  8.21 us (11%)
  local copies, waits for them, and re-layouts  1.59 us (2%)
    all_to_all x3, starting transfers between devices, to_each(): lax.all_to_all(tiles, axis, split_axis=0, concat_axis=0, tiled=True, axis...  34.7 us
    all_gather x1, blocking collectives, on_device(): lax.all_gather(left, 'col', axis=0, tiled=True, axis_index_groups=[chip_r...  15.7 us
    all_to_all x3, waiting for transfers between devices, to_each(): lax.all_to_all(tiles, axis, split_axis=0, concat_axis=0, tiled=True, axis...  9.46 us
    pallas_call x6, Pallas kernels, on_core(): pl.pallas_call(kernel, out_shape=[jax.ShapeDtypeStruct(*out) for out in o...  8.21 us
    ppermute x1, starting transfers between devices, on_device(): lax.ppermute(away, 'row', [(k, (k + half) % owners) for k in range(owners)])  4.55 us
  transfers between devices with their start and end apart: 4, of which 2 were waited for; matrix products, arithmetic and copies ran while one was open for 0% of the time, Pallas kernels for 5%

profile of v5, /device:TPU:1, one launch (start us, length us, event | category | flops | bytes accessed | tf_op | source)
XLA Modules:
  0.0 74.9 jit_solution(593662075819128733)
XLA Ops:
  0.6 1.5 %broadcast_in_dim.3 = bf16[32,4,1024]{2,1,0:T(4,128)(2,1)} broadcast(bf16[4,1024]{1,0:T(4,128)(2,1)} %param.10), dimensions={1,2} | broadcast | bytes 270336 | tf_op jit(solution)/shard_map/broadcast_in_dim | solution.py:196
  2.1 19.2 %all-to-all-start = ((bf16[32,4,1024]{2,1,0:T(4,128)(2,1)}), bf16[32,4,1024]{2,1,0:T(4,128)(2,1)S(1)}, u32[]{:S(2)}, u32[]{:S(2)}) async-start(bf16[32,4,1024]{2,1,0:T(4,128)(2,1)} %broadcast_in_dim.3), calls=%async_computation | async-start | bytes 524288 | tf_op jit(solution)/shard_map/all_to_all | solution.py:182
  21.3 0.0 copy-done.5
  21.3 0.0 copy-start.2
  21.3 15.7 %all_gather.3.left = bf16[128,512]{1,0:T(8,128)(2,1)S(1)} all-gather(bf16[8,512]{1,0:T(8,128)(2,1)S(1)} %copy-done.5), channel_id=1, replica_groups={{0,1,4,5,8,9,12,13,14,15,10,11,6,7,2,3},{16,17,20,21,24,25,28,29,30,31,..., dimensions={0}, use_global_device_ids=true | all-gather | bytes 139264 | tf_op jit(solution)/shard_map/all_gather | solution.py:198
  37.0 0.0 copy-done.3
  37.0 0.0 copy-done.2
  37.0 0.0 copy-start
  37.1 0.0 copy-start.1
  37.1 0.8 %shard_map.112 = (bf16[512,128]{1,0:T(8,128)(2,1)S(1)}, bf16[128,512]{1,0:T(8,128)(2,1)S(1)}, bf16[512,128]{1,0:T(8,128)(2,1)S(1)}, bf16[512,128]{1,0:T(8,128)(2,1)S(1)}, bf16[512,512]{1,0:T(8,128)(2,1)S(1)}) custom-call(bf16[128,512]{1,0:T(8,128)(2,1)S(1)} %all_gather.3.left, bf16[16,32,128]{2,1,0:T(8,128)(2,1)S(1)} %copy-done.2, ...), custom_call_target="tpu_custom_call" | custom-call | flops 400000000 | bytes 2000000 | tf_op jit(solution)/shard_map/pallas_call | solution.py:168
  37.9 0.0 all-to-all-done.right
  37.9 0.1 copy-done
  38.0 0.0 copy-done.1
  38.0 3.8 %shard_map.113 = (bf16[64,1024]{1,0:T(8,128)(2,1)S(1)}, f32[64,1024]{1,0:T(8,128)S(1)}, f32[512,128]{1,0:T(8,128)S(1)}, bf16[512,512]{1,0:T(8,128)(2,1)S(1)}, bf16[128,512]{1,0:T(8,128)(2,1)}) custom-call(bf16[32,4,1024]{2,1,0:T(4,128)(2,1)S(1)} %all-to-all-done.right, bf16[512,128]{1,0:T(8,128)(2,1)S(1)} %get-tuple-element.13.left_t, ...), custom_call_target="tpu_custom_call" | custom-call | flops 400000000 | bytes 2000000 | tf_op jit(solution)/shard_map/pallas_call | solution.py:168
  41.8 4.5 %collective-permute-start = (bf16[64,1024]{1,0:T(8,128)(2,1)S(1)}, bf16[64,1024]{1,0:T(8,128)(2,1)S(1)}, u32[]{:S(2)}, u32[]{:S(2)}) collective-permute-start(bf16[64,1024]{1,0:T(8,128)(2,1)S(1)} %get-tuple-element.22), channel_id=1, source_target_pairs={{0,256},{16,272},{32,288},{48,304},{64,320},{80,336},{96,352},{112... | collective-permute-start | bytes 393224 | tf_op jit(solution)/shard_map/ppermute | solution.py:238
  46.4 4.0 %all-to-all-start.1 = ((bf16[16,8,512]{2,1,0:T(8,128)(2,1)}), bf16[16,8,512]{2,1,0:T(8,128)(2,1)S(1)}, u32[]{:S(2)}, u32[]{:S(2)}) async-start(bf16[16,8,512]{2,1,0:T(8,128)(2,1)} %bitcast.2), calls=%async_computation.1 | async-start | bytes 262144 | tf_op jit(solution)/shard_map/all_to_all | solution.py:182
  50.4 0.0 collective-permute-done.came
  50.4 0.7 shard_map.116
  51.1 5.4 %all-to-all-done.1.arrived = bf16[16,8,512]{2,1,0:T(8,128)(2,1)S(1)} async-done(((bf16[16,8,512]{2,1,0:T(8,128)(2,1)}), bf16[16,8,512]{2,1,0:T(8,128)(2,1)S(1)}, u32[]{:S(2)}, u32[]{:S(2)}) %all-to-all-start.1) | async-done | bytes 131104 | tf_op jit(solution)/shard_map/all_to_all | solution.py:182
  56.5 11.5 %all-to-all-start.2 = ((bf16[16,4,1024]{2,1,0:T(4,128)(2,1)}), bf16[16,4,1024]{2,1,0:T(4,128)(2,1)S(1)}, u32[]{:S(2)}, u32[]{:S(2)}) async-start(bf16[16,4,1024]{2,1,0:T(4,128)(2,1)} %shard_map.116), calls=%async_computation.2 | async-start | bytes 262144 | tf_op jit(solution)/shard_map/all_to_all | solution.py:182
  68.0 1.4 %shard_map.114 = bf16[16,32,128]{2,1,0:T(8,128)(2,1)} custom-call(f32[512,128]{1,0:T(8,128)S(1)} %get-tuple-element.18.middle, bf16[512,512]{1,0:T(8,128)(2,1)S(1)} %get-tuple-element.19.hidden, bf16[512,128]{1,0:T(8,128)(2,1)S(1)} %copy-done.4), custom_call_target="tpu_custom_call" | custom-call | flops 400000000 | bytes 2000000 | tf_op jit(solution)/shard_map/pallas_call | solution.py:168
  69.4 0.8 %shard_map.115 = bf16[8,512]{1,0:T(8,128)(2,1)} custom-call(bf16[16,8,512]{2,1,0:T(8,128)(2,1)S(1)} %all-to-all-done.1.arrived), custom_call_target="tpu_custom_call" | custom-call | flops 400000000 | bytes 2000000 | tf_op jit(solution)/shard_map/pallas_call | solution.py:168
  70.3 4.0 %all-to-all-done.2.arrived = bf16[16,4,1024]{2,1,0:T(4,128)(2,1)S(1)} async-done(((bf16[16,4,1024]{2,1,0:T(4,128)(2,1)}), bf16[16,4,1024]{2,1,0:T(4,128)(2,1)S(1)}, u32[]{:S(2)}, u32[]{:S(2)}) %all-to-all-start.2) | async-done | bytes 131104 | tf_op jit(solution)/shard_map/all_to_all | solution.py:182
  74.3 0.7 shard_map.117
  (4 shorter events, 0.0 us)
Async XLA Ops:
  2.1 19.2 %copy-start.5 = (bf16[8,512]{1,0:T(8,128)(2,1)S(1)}, bf16[8,512]{1,0:T(8,128)(2,1)}, u32[]{:S(2)}) copy-start(bf16[8,512]{1,0:T(8,128)(2,1)} %param.9) | copy-start | bytes 24580
  2.1 34.9 %copy-start.3 = (bf16[16,32,128]{2,1,0:T(8,128)(2,1)S(1)}, bf16[16,32,128]{2,1,0:T(8,128)(2,1)}, u32[]{:S(2)}) copy-start(bf16[16,32,128]{2,1,0:T(8,128)(2,1)} %pair_cot.1) | copy-start | bytes 393220
  2.1 34.9 %copy-start.4 = (bf16[512,128]{1,0:T(8,128)(2,1)S(1)}, bf16[512,128]{1,0:T(8,128)(2,1)}, u32[]{:S(2)}) copy-start(bf16[512,128]{1,0:T(8,128)(2,1)} %down.3) | copy-start | bytes 393220
  2.1 35.8 %all-to-all-start = ((bf16[32,4,1024]{2,1,0:T(4,128)(2,1)}), bf16[32,4,1024]{2,1,0:T(4,128)(2,1)S(1)}, u32[]{:S(2)}, u32[]{:S(2)}) async-start(bf16[32,4,1024]{2,1,0:T(4,128)(2,1)} %broadcast_in_dim.3), calls=%async_computation | async-start | bytes 524288 | tf_op jit(solution)/shard_map/all_to_all | solution.py:182
  21.3 15.8 %copy-start.2 = (bf16[16,32,128]{2,1,0:T(8,128)(2,1)S(1)}, bf16[16,32,128]{2,1,0:T(8,128)(2,1)}, u32[]{:S(2)}) copy-start(bf16[16,32,128]{2,1,0:T(8,128)(2,1)} %pair_in.1) | copy-start | bytes 393220
  37.0 1.0 %copy-start = (bf16[1024,128]{1,0:T(8,128)(2,1)S(1)}, bf16[1024,128]{1,0:T(8,128)(2,1)}, u32[]{:S(2)}) copy-start(bf16[1024,128]{1,0:T(8,128)(2,1)} %weight.1) | copy-start | bytes 786436
  37.1 1.0 %copy-start.1 = (bf16[128,512]{1,0:T(8,128)(2,1)S(1)}, bf16[128,512]{1,0:T(8,128)(2,1)}, u32[]{:S(2)}) copy-start(bf16[128,512]{1,0:T(8,128)(2,1)} %up.1) | copy-start | bytes 393220
  41.8 8.6 %collective-permute-start = (bf16[64,1024]{1,0:T(8,128)(2,1)S(1)}, bf16[64,1024]{1,0:T(8,128)(2,1)S(1)}, u32[]{:S(2)}, u32[]{:S(2)}) collective-permute-start(bf16[64,1024]{1,0:T(8,128)(2,1)S(1)} %get-tuple-element.22), channel_id=1, source_target_pairs={{0,256},{16,272},{32,288},{48,304},{64,320},{80,336},{96,352},{112... | collective-permute-start | bytes 393224 | tf_op jit(solution)/shard_map/ppermute | solution.py:238
  46.4 10.2 %all-to-all-start.1 = ((bf16[16,8,512]{2,1,0:T(8,128)(2,1)}), bf16[16,8,512]{2,1,0:T(8,128)(2,1)S(1)}, u32[]{:S(2)}, u32[]{:S(2)}) async-start(bf16[16,8,512]{2,1,0:T(8,128)(2,1)} %bitcast.2), calls=%async_computation.1 | async-start | bytes 262144 | tf_op jit(solution)/shard_map/all_to_all | solution.py:182
  56.5 17.8 %all-to-all-start.2 = ((bf16[16,4,1024]{2,1,0:T(4,128)(2,1)}), bf16[16,4,1024]{2,1,0:T(4,128)(2,1)S(1)}, u32[]{:S(2)}, u32[]{:S(2)}) async-start(bf16[16,4,1024]{2,1,0:T(4,128)(2,1)} %shard_map.116), calls=%async_computation.2 | async-start | bytes 262144 | tf_op jit(solution)/shard_map/all_to_all | solution.py:182

commit v6 on v5

--- a/solution.py
+++ b/solution.py
@@ -11,7 +11,7 @@
 F32 = jnp.float32
 BF16 = jnp.bfloat16
 Y, X, CORES = 4, 2, 2
-OUT, BACK = (11, 1), (8, 7)
+OUT, BACK = (11, 7), (9, 7)
 NN = (((1,), (0,)), ((), ()))
 NT = (((1,), (1,)), ((), ()))
 TN = (((0,), (0,)), ((), ()))
@@ -94,7 +94,7 @@
     owners, each, width = right.shape
     rows = left_t.shape[0] // C
     for k, z in enumerate(listed(owners // 2, OUT)):
-        for at, block in ((z, k), (z + owners // 2, k + owners // 2)):
+        for at, block in ((z, 2 * k), (z + owners // 2, 2 * k + 1)):
             tall[at * each : (at + 1) * each, :] = right[block].astype(F32)
     right_all[...] = tall[: owners * each, :].astype(BF16)
     tall[...] = mm(left_t[...], right_all[...])
@@ -194,7 +194,7 @@
         [[start + z for z in listed(half, order)] for start in (0, half)] for order in (OUT, BACK)
     )
     copies = jnp.broadcast_to(right, (owners, *right.shape))
-    right_blocks = to_each(copies, "row", [out_order[0] + out_order[1]])
+    right_blocks = to_each(copies, "row", [[k for pair in zip(*out_order) for k in pair]])
     left_blocks = lax.all_gather(
         left, "col", axis=0, tiled=True, axis_index_groups=[chip_ring()]
     )

time: 76 us -> 75.9 us (level)
  no operation moved by 1% of the time
where the time goes in v6:
time: 75.9 us; the launch traced here: 75.4 us
  starting transfers between devices  39.1 us (52%)
  blocking collectives  15.7 us (21%)
  waiting for transfers between devices  10.1 us (13%)
  Pallas kernels  8.2 us (11%)
  local copies, waits for them, and re-layouts  1.59 us (2%)
    all_to_all x3, starting transfers between devices, to_each(): lax.all_to_all(tiles, axis, split_axis=0, concat_axis=0, tiled=True, axis...  34.6 us
    all_gather x1, blocking collectives, on_device(): lax.all_gather(left, 'col', axis=0, tiled=True, axis_index_groups=[chip_r...  15.7 us
    all_to_all x3, waiting for transfers between devices, to_each(): lax.all_to_all(tiles, axis, split_axis=0, concat_axis=0, tiled=True, axis...  10.1 us
    pallas_call x6, Pallas kernels, on_core(): pl.pallas_call(kernel, out_shape=[jax.ShapeDtypeStruct(*out) for out in o...  8.2 us
    ppermute x1, starting transfers between devices, on_device(): lax.ppermute(away, 'row', [(k, (k + half) % owners) for k in range(owners)])  4.59 us
  transfers between devices with their start and end apart: 4, of which 2 were waited for; matrix products, arithmetic and copies ran while one was open for 0% of the time, Pallas kernels for 5%

profile of v6, /device:TPU:1, one launch (start us, length us, event | category | flops | bytes accessed | tf_op | source)
XLA Modules:
  0.0 75.4 jit_solution(7505270265637048961)
XLA Ops:
  0.6 1.5 %broadcast_in_dim.3 = bf16[32,4,1024]{2,1,0:T(4,128)(2,1)} broadcast(bf16[4,1024]{1,0:T(4,128)(2,1)} %param.10), dimensions={1,2} | broadcast | bytes 270336 | tf_op jit(solution)/shard_map/broadcast_in_dim | solution.py:196
  2.1 19.2 %all-to-all-start = ((bf16[32,4,1024]{2,1,0:T(4,128)(2,1)}), bf16[32,4,1024]{2,1,0:T(4,128)(2,1)S(1)}, u32[]{:S(2)}, u32[]{:S(2)}) async-start(bf16[32,4,1024]{2,1,0:T(4,128)(2,1)} %broadcast_in_dim.3), calls=%async_computation | async-start | bytes 524288 | tf_op jit(solution)/shard_map/all_to_all | solution.py:182
  21.3 0.0 copy-done.5
  21.3 0.0 copy-start.2
  21.3 15.7 %all_gather.3.left = bf16[128,512]{1,0:T(8,128)(2,1)S(1)} all-gather(bf16[8,512]{1,0:T(8,128)(2,1)S(1)} %copy-done.5), channel_id=1, replica_groups={{0,1,4,5,8,9,12,13,14,15,10,11,6,7,2,3},{16,17,20,21,24,25,28,29,30,31,..., dimensions={0}, use_global_device_ids=true | all-gather | bytes 139264 | tf_op jit(solution)/shard_map/all_gather | solution.py:198
  37.0 0.0 copy-done.3
  37.0 0.0 copy-done.4
  37.0 0.0 copy-start
  37.0 0.0 copy-start.1
  37.0 0.9 %shard_map.112 = (bf16[512,128]{1,0:T(8,128)(2,1)S(1)}, bf16[128,512]{1,0:T(8,128)(2,1)S(1)}, bf16[512,128]{1,0:T(8,128)(2,1)S(1)}, bf16[512,128]{1,0:T(8,128)(2,1)S(1)}, bf16[512,512]{1,0:T(8,128)(2,1)S(1)}) custom-call(bf16[128,512]{1,0:T(8,128)(2,1)S(1)} %all_gather.3.left, bf16[16,32,128]{2,1,0:T(8,128)(2,1)S(1)} %copy-done.2, ...), custom_call_target="tpu_custom_call" | custom-call | flops 400000000 | bytes 2000000 | tf_op jit(solution)/shard_map/pallas_call | solution.py:168
  37.9 0.0 all-to-all-done.right
  37.9 0.1 copy-done
  37.9 0.0 copy-done.1
  38.0 3.8 %shard_map.113 = (bf16[64,1024]{1,0:T(8,128)(2,1)S(1)}, f32[64,1024]{1,0:T(8,128)S(1)}, f32[512,128]{1,0:T(8,128)S(1)}, bf16[512,512]{1,0:T(8,128)(2,1)S(1)}, bf16[128,512]{1,0:T(8,128)(2,1)}) custom-call(bf16[32,4,1024]{2,1,0:T(4,128)(2,1)S(1)} %all-to-all-done.right, bf16[512,128]{1,0:T(8,128)(2,1)S(1)} %get-tuple-element.13.left_t, ...), custom_call_target="tpu_custom_call" | custom-call | flops 400000000 | bytes 2000000 | tf_op jit(solution)/shard_map/pallas_call | solution.py:168
  41.7 4.6 %collective-permute-start = (bf16[64,1024]{1,0:T(8,128)(2,1)S(1)}, bf16[64,1024]{1,0:T(8,128)(2,1)S(1)}, u32[]{:S(2)}, u32[]{:S(2)}) collective-permute-start(bf16[64,1024]{1,0:T(8,128)(2,1)S(1)} %get-tuple-element.22), channel_id=1, source_target_pairs={{0,256},{16,272},{32,288},{48,304},{64,320},{80,336},{96,352},{112... | collective-permute-start | bytes 393224 | tf_op jit(solution)/shard_map/ppermute | solution.py:238
  46.3 3.9 %all-to-all-start.1 = ((bf16[16,8,512]{2,1,0:T(8,128)(2,1)}), bf16[16,8,512]{2,1,0:T(8,128)(2,1)S(1)}, u32[]{:S(2)}, u32[]{:S(2)}) async-start(bf16[16,8,512]{2,1,0:T(8,128)(2,1)} %bitcast.2), calls=%async_computation.1 | async-start | bytes 262144 | tf_op jit(solution)/shard_map/all_to_all | solution.py:182
  50.2 0.0 collective-permute-done.came
  50.2 0.7 shard_map.116
  50.9 5.4 %all-to-all-done.1.arrived = bf16[16,8,512]{2,1,0:T(8,128)(2,1)S(1)} async-done(((bf16[16,8,512]{2,1,0:T(8,128)(2,1)}), bf16[16,8,512]{2,1,0:T(8,128)(2,1)S(1)}, u32[]{:S(2)}, u32[]{:S(2)}) %all-to-all-start.1) | async-done | bytes 131104 | tf_op jit(solution)/shard_map/all_to_all | solution.py:182
  56.3 11.5 %all-to-all-start.2 = ((bf16[16,4,1024]{2,1,0:T(4,128)(2,1)}), bf16[16,4,1024]{2,1,0:T(4,128)(2,1)S(1)}, u32[]{:S(2)}, u32[]{:S(2)}) async-start(bf16[16,4,1024]{2,1,0:T(4,128)(2,1)} %shard_map.116), calls=%async_computation.2 | async-start | bytes 262144 | tf_op jit(solution)/shard_map/all_to_all | solution.py:182
  67.9 1.4 %shard_map.114 = bf16[16,32,128]{2,1,0:T(8,128)(2,1)} custom-call(f32[512,128]{1,0:T(8,128)S(1)} %get-tuple-element.18.middle, bf16[512,512]{1,0:T(8,128)(2,1)S(1)} %get-tuple-element.19.hidden, bf16[512,128]{1,0:T(8,128)(2,1)S(1)} %copy-done.4), custom_call_target="tpu_custom_call" | custom-call | flops 400000000 | bytes 2000000 | tf_op jit(solution)/shard_map/pallas_call | solution.py:168
  69.3 0.8 %shard_map.115 = bf16[8,512]{1,0:T(8,128)(2,1)} custom-call(bf16[16,8,512]{2,1,0:T(8,128)(2,1)S(1)} %all-to-all-done.1.arrived), custom_call_target="tpu_custom_call" | custom-call | flops 400000000 | bytes 2000000 | tf_op jit(solution)/shard_map/pallas_call | solution.py:168
  70.1 4.6 %all-to-all-done.2.arrived = bf16[16,4,1024]{2,1,0:T(4,128)(2,1)S(1)} async-done(((bf16[16,4,1024]{2,1,0:T(4,128)(2,1)}), bf16[16,4,1024]{2,1,0:T(4,128)(2,1)S(1)}, u32[]{:S(2)}, u32[]{:S(2)}) %all-to-all-start.2) | async-done | bytes 131104 | tf_op jit(solution)/shard_map/all_to_all | solution.py:182
  74.7 0.7 shard_map.117
  (4 shorter events, 0.0 us)
Async XLA Ops:
  2.1 19.2 %copy-start.5 = (bf16[8,512]{1,0:T(8,128)(2,1)S(1)}, bf16[8,512]{1,0:T(8,128)(2,1)}, u32[]{:S(2)}) copy-start(bf16[8,512]{1,0:T(8,128)(2,1)} %param.9) | copy-start | bytes 24580
  2.1 34.9 %copy-start.3 = (bf16[16,32,128]{2,1,0:T(8,128)(2,1)S(1)}, bf16[16,32,128]{2,1,0:T(8,128)(2,1)}, u32[]{:S(2)}) copy-start(bf16[16,32,128]{2,1,0:T(8,128)(2,1)} %pair_cot.1) | copy-start | bytes 393220
  2.1 34.9 %copy-start.4 = (bf16[512,128]{1,0:T(8,128)(2,1)S(1)}, bf16[512,128]{1,0:T(8,128)(2,1)}, u32[]{:S(2)}) copy-start(bf16[512,128]{1,0:T(8,128)(2,1)} %down.3) | copy-start | bytes 393220
  2.1 35.8 %all-to-all-start = ((bf16[32,4,1024]{2,1,0:T(4,128)(2,1)}), bf16[32,4,1024]{2,1,0:T(4,128)(2,1)S(1)}, u32[]{:S(2)}, u32[]{:S(2)}) async-start(bf16[32,4,1024]{2,1,0:T(4,128)(2,1)} %broadcast_in_dim.3), calls=%async_computation | async-start | bytes 524288 | tf_op jit(solution)/shard_map/all_to_all | solution.py:182
  21.3 15.7 %copy-start.2 = (bf16[16,32,128]{2,1,0:T(8,128)(2,1)S(1)}, bf16[16,32,128]{2,1,0:T(8,128)(2,1)}, u32[]{:S(2)}) copy-start(bf16[16,32,128]{2,1,0:T(8,128)(2,1)} %pair_in.1) | copy-start | bytes 393220
  37.0 1.0 %copy-start = (bf16[1024,128]{1,0:T(8,128)(2,1)S(1)}, bf16[1024,128]{1,0:T(8,128)(2,1)}, u32[]{:S(2)}) copy-start(bf16[1024,128]{1,0:T(8,128)(2,1)} %weight.1) | copy-start | bytes 786436
  37.0 1.0 %copy-start.1 = (bf16[128,512]{1,0:T(8,128)(2,1)S(1)}, bf16[128,512]{1,0:T(8,128)(2,1)}, u32[]{:S(2)}) copy-start(bf16[128,512]{1,0:T(8,128)(2,1)} %up.1) | copy-start | bytes 393220
  41.7 8.5 %collective-permute-start = (bf16[64,1024]{1,0:T(8,128)(2,1)S(1)}, bf16[64,1024]{1,0:T(8,128)(2,1)S(1)}, u32[]{:S(2)}, u32[]{:S(2)}) collective-permute-start(bf16[64,1024]{1,0:T(8,128)(2,1)S(1)} %get-tuple-element.22), channel_id=1, source_target_pairs={{0,256},{16,272},{32,288},{48,304},{64,320},{80,336},{96,352},{112... | collective-permute-start | bytes 393224 | tf_op jit(solution)/shard_map/ppermute | solution.py:238
  46.3 10.0 %all-to-all-start.1 = ((bf16[16,8,512]{2,1,0:T(8,128)(2,1)}), bf16[16,8,512]{2,1,0:T(8,128)(2,1)S(1)}, u32[]{:S(2)}, u32[]{:S(2)}) async-start(bf16[16,8,512]{2,1,0:T(8,128)(2,1)} %bitcast.2), calls=%async_computation.1 | async-start | bytes 262144 | tf_op jit(solution)/shard_map/all_to_all | solution.py:182
  56.3 18.4 %all-to-all-start.2 = ((bf16[16,4,1024]{2,1,0:T(4,128)(2,1)}), bf16[16,4,1024]{2,1,0:T(4,128)(2,1)S(1)}, u32[]{:S(2)}, u32[]{:S(2)}) async-start(bf16[16,4,1024]{2,1,0:T(4,128)(2,1)} %shard_map.116), calls=%async_computation.2 | async-start | bytes 262144 | tf_op jit(solution)/shard_map/all_to_all | solution.py:182

commit v7 on v6

--- a/solution.py
+++ b/solution.py
@@ -59,13 +59,12 @@
     rows, cols, _ = pair_in.shape
     swap = swap_rows(C, rows)
     swap_pair = swap if cols == C else swap_rows(cols, rows)
+    left_t[...] = mm(swap, left[...], NT).astype(BF16)
     ring = chip_ring()
     each = left.shape[0] // len(ring)
-    came = left[...].astype(F32)
-    blocks = [came[ring.index(k) * each : (ring.index(k) + 1) * each] for k in range(len(ring))]
-    left_all = jnp.concatenate(blocks, axis=0).astype(BF16)
-    left_t[...] = mm(swap, left_all, NT).astype(BF16)
-    left_p[...] = mm(left_all, swap, NT).astype(BF16)
+    turned = mm(left[...], swap, NT)
+    blocks = [turned[ring.index(k) * each : (ring.index(k) + 1) * each] for k in range(len(ring))]
+    left_p[...] = jnp.concatenate(blocks, axis=0).astype(BF16)
     pair_p[...] = mm(swap_pair, pair_in[...].reshape(rows * cols, -1)).astype(BF16)
     cot = mm(swap_pair, pair_cot[...].reshape(rows * cols, -1)).astype(BF16)
     cot_p[...] = cot
@@ -93,9 +92,12 @@
     fetch_bias.start()
     owners, each, width = right.shape
     rows = left_t.shape[0] // C
+    ring = chip_ring()
+    share = owners // len(ring)
     for k, z in enumerate(listed(owners // 2, OUT)):
         for at, block in ((z, 2 * k), (z + owners // 2, 2 * k + 1)):
-            tall[at * each : (at + 1) * each, :] = right[block].astype(F32)
+            row = ring.index(at // share) * share * each + at % share * each
+            tall[row : row + each, :] = right[block].astype(F32)
     right_all[...] = tall[: owners * each, :].astype(BF16)
     tall[...] = mm(left_t[...], right_all[...])
     regroup(tall, outer, rows, 1.0 / SEQS)
@@ -236,7 +238,7 @@
         far_out=1,
     )
     came = lax.ppermute(away, "row", [(k, (k + half) % owners) for k in range(owners)])
-    left_tiles = to_each(grad_left.reshape(-1, *left.shape), "col")
+    left_tiles = to_each(grad_left.reshape(-1, *left.shape), "col", [chip_ring()])
     (tiles,) = on_core(
         join_halves, [kept, came], [((half, *right.shape), BF16)], [((SEQS // 2, right_size), F32)]
     )

time: 75.9 us -> 76.3 us (level)
  no operation moved by 1% of the time
where the time goes in v7:
time: 76.3 us; the launch traced here: 75.8 us
  starting transfers between devices  39.1 us (51%)
  blocking collectives  15.7 us (21%)
  waiting for transfers between devices  10.5 us (14%)
  Pallas kernels  8.21 us (11%)
  local copies, waits for them, and re-layouts  1.59 us (2%)
    all_to_all x3, starting transfers between devices, to_each(): lax.all_to_all(tiles, axis, split_axis=0, concat_axis=0, tiled=True, axis...  34.5 us
    all_gather x1, blocking collectives, on_device(): lax.all_gather(left, 'col', axis=0, tiled=True, axis_index_groups=[chip_r...  15.7 us
    all_to_all x3, waiting for transfers between devices, to_each(): lax.all_to_all(tiles, axis, split_axis=0, concat_axis=0, tiled=True, axis...  10.5 us
    pallas_call x6, Pallas kernels, on_core(): pl.pallas_call(kernel, out_shape=[jax.ShapeDtypeStruct(*out) for out in o...  8.21 us
    ppermute x1, starting transfers between devices, on_device(): lax.ppermute(away, 'row', [(k, (k + half) % owners) for k in range(owners)])  4.59 us
  transfers between devices with their start and end apart: 4, of which 2 were waited for; matrix products, arithmetic and copies ran while one was open for 0% of the time, Pallas kernels for 5%

profile of v7, /device:TPU:1, one launch (start us, length us, event | category | flops | bytes accessed | tf_op | source)
XLA Modules:
  0.0 75.8 jit_solution(1784404148274219586)
XLA Ops:
  0.6 1.5 %broadcast_in_dim.3 = bf16[32,4,1024]{2,1,0:T(4,128)(2,1)} broadcast(bf16[4,1024]{1,0:T(4,128)(2,1)} %param.10), dimensions={1,2} | broadcast | bytes 270336 | tf_op jit(solution)/shard_map/broadcast_in_dim | solution.py:198
  2.1 19.2 %all-to-all-start = ((bf16[32,4,1024]{2,1,0:T(4,128)(2,1)}), bf16[32,4,1024]{2,1,0:T(4,128)(2,1)S(1)}, u32[]{:S(2)}, u32[]{:S(2)}) async-start(bf16[32,4,1024]{2,1,0:T(4,128)(2,1)} %broadcast_in_dim.3), calls=%async_computation | async-start | bytes 524288 | tf_op jit(solution)/shard_map/all_to_all | solution.py:184
  21.3 0.0 copy-done.5
  21.3 0.0 copy-start.2
  21.3 15.7 %all_gather.3.left = bf16[128,512]{1,0:T(8,128)(2,1)S(1)} all-gather(bf16[8,512]{1,0:T(8,128)(2,1)S(1)} %copy-done.5), channel_id=1, replica_groups={{0,1,4,5,8,9,12,13,14,15,10,11,6,7,2,3},{16,17,20,21,24,25,28,29,30,31,..., dimensions={0}, use_global_device_ids=true | all-gather | bytes 139264 | tf_op jit(solution)/shard_map/all_gather | solution.py:200
  37.0 0.0 copy-done.3
  37.0 0.0 copy-done.4
  37.0 0.0 copy-start
  37.0 0.0 copy-start.1
  37.0 0.9 %shard_map.112 = (bf16[512,128]{1,0:T(8,128)(2,1)S(1)}, bf16[128,512]{1,0:T(8,128)(2,1)S(1)}, bf16[512,128]{1,0:T(8,128)(2,1)S(1)}, bf16[512,128]{1,0:T(8,128)(2,1)S(1)}, bf16[512,512]{1,0:T(8,128)(2,1)S(1)}) custom-call(bf16[128,512]{1,0:T(8,128)(2,1)S(1)} %all_gather.3.left, bf16[16,32,128]{2,1,0:T(8,128)(2,1)S(1)} %copy-done.2, ...), custom_call_target="tpu_custom_call" | custom-call | flops 400000000 | bytes 2000000 | tf_op jit(solution)/shard_map/pallas_call | solution.py:170
  37.9 0.0 all-to-all-done.right
  37.9 0.1 copy-done
  37.9 0.0 copy-done.1
  38.0 3.8 %shard_map.113 = (bf16[64,1024]{1,0:T(8,128)(2,1)S(1)}, f32[64,1024]{1,0:T(8,128)S(1)}, f32[512,128]{1,0:T(8,128)S(1)}, bf16[512,512]{1,0:T(8,128)(2,1)S(1)}, bf16[128,512]{1,0:T(8,128)(2,1)}) custom-call(bf16[32,4,1024]{2,1,0:T(4,128)(2,1)S(1)} %all-to-all-done.right, bf16[512,128]{1,0:T(8,128)(2,1)S(1)} %get-tuple-element.13.left_t, ...), custom_call_target="tpu_custom_call" | custom-call | flops 400000000 | bytes 2000000 | tf_op jit(solution)/shard_map/pallas_call | solution.py:170
  41.7 4.6 %collective-permute-start = (bf16[64,1024]{1,0:T(8,128)(2,1)S(1)}, bf16[64,1024]{1,0:T(8,128)(2,1)S(1)}, u32[]{:S(2)}, u32[]{:S(2)}) collective-permute-start(bf16[64,1024]{1,0:T(8,128)(2,1)S(1)} %get-tuple-element.22), channel_id=1, source_target_pairs={{0,256},{16,272},{32,288},{48,304},{64,320},{80,336},{96,352},{112... | collective-permute-start | bytes 393224 | tf_op jit(solution)/shard_map/ppermute | solution.py:240
  46.3 3.9 %all-to-all-start.1 = ((bf16[16,8,512]{2,1,0:T(8,128)(2,1)}), bf16[16,8,512]{2,1,0:T(8,128)(2,1)S(1)}, u32[]{:S(2)}, u32[]{:S(2)}) async-start(bf16[16,8,512]{2,1,0:T(8,128)(2,1)} %bitcast.2), calls=%async_computation.1 | async-start | bytes 262144 | tf_op jit(solution)/shard_map/all_to_all | solution.py:184
  50.2 0.0 collective-permute-done.came
  50.2 0.7 shard_map.116
  50.9 5.4 %all-to-all-done.1.arrived = bf16[16,8,512]{2,1,0:T(8,128)(2,1)S(1)} async-done(((bf16[16,8,512]{2,1,0:T(8,128)(2,1)}), bf16[16,8,512]{2,1,0:T(8,128)(2,1)S(1)}, u32[]{:S(2)}, u32[]{:S(2)}) %all-to-all-start.1) | async-done | bytes 131104 | tf_op jit(solution)/shard_map/all_to_all | solution.py:184
  56.3 11.5 %all-to-all-start.2 = ((bf16[16,4,1024]{2,1,0:T(4,128)(2,1)}), bf16[16,4,1024]{2,1,0:T(4,128)(2,1)S(1)}, u32[]{:S(2)}, u32[]{:S(2)}) async-start(bf16[16,4,1024]{2,1,0:T(4,128)(2,1)} %shard_map.116), calls=%async_computation.2 | async-start | bytes 262144 | tf_op jit(solution)/shard_map/all_to_all | solution.py:184
  67.8 1.4 %shard_map.114 = bf16[16,32,128]{2,1,0:T(8,128)(2,1)} custom-call(f32[512,128]{1,0:T(8,128)S(1)} %get-tuple-element.18.middle, bf16[512,512]{1,0:T(8,128)(2,1)S(1)} %get-tuple-element.19.hidden, bf16[512,128]{1,0:T(8,128)(2,1)S(1)} %copy-done.4), custom_call_target="tpu_custom_call" | custom-call | flops 400000000 | bytes 2000000 | tf_op jit(solution)/shard_map/pallas_call | solution.py:170
  69.2 0.8 %shard_map.115 = bf16[8,512]{1,0:T(8,128)(2,1)} custom-call(bf16[16,8,512]{2,1,0:T(8,128)(2,1)S(1)} %all-to-all-done.1.arrived), custom_call_target="tpu_custom_call" | custom-call | flops 400000000 | bytes 2000000 | tf_op jit(solution)/shard_map/pallas_call | solution.py:170
  70.0 5.1 %all-to-all-done.2.arrived = bf16[16,4,1024]{2,1,0:T(4,128)(2,1)S(1)} async-done(((bf16[16,4,1024]{2,1,0:T(4,128)(2,1)}), bf16[16,4,1024]{2,1,0:T(4,128)(2,1)S(1)}, u32[]{:S(2)}, u32[]{:S(2)}) %all-to-all-start.2) | async-done | bytes 131104 | tf_op jit(solution)/shard_map/all_to_all | solution.py:184
  75.1 0.7 shard_map.117
  (4 shorter events, 0.0 us)
Async XLA Ops:
  2.1 19.2 %copy-start.5 = (bf16[8,512]{1,0:T(8,128)(2,1)S(1)}, bf16[8,512]{1,0:T(8,128)(2,1)}, u32[]{:S(2)}) copy-start(bf16[8,512]{1,0:T(8,128)(2,1)} %param.9) | copy-start | bytes 24580
  2.1 34.9 %copy-start.3 = (bf16[16,32,128]{2,1,0:T(8,128)(2,1)S(1)}, bf16[16,32,128]{2,1,0:T(8,128)(2,1)}, u32[]{:S(2)}) copy-start(bf16[16,32,128]{2,1,0:T(8,128)(2,1)} %pair_cot.1) | copy-start | bytes 393220
  2.1 34.9 %copy-start.4 = (bf16[512,128]{1,0:T(8,128)(2,1)S(1)}, bf16[512,128]{1,0:T(8,128)(2,1)}, u32[]{:S(2)}) copy-start(bf16[512,128]{1,0:T(8,128)(2,1)} %down.3) | copy-start | bytes 393220
  2.1 35.8 %all-to-all-start = ((bf16[32,4,1024]{2,1,0:T(4,128)(2,1)}), bf16[32,4,1024]{2,1,0:T(4,128)(2,1)S(1)}, u32[]{:S(2)}, u32[]{:S(2)}) async-start(bf16[32,4,1024]{2,1,0:T(4,128)(2,1)} %broadcast_in_dim.3), calls=%async_computation | async-start | bytes 524288 | tf_op jit(solution)/shard_map/all_to_all | solution.py:184
  21.3 15.7 %copy-start.2 = (bf16[16,32,128]{2,1,0:T(8,128)(2,1)S(1)}, bf16[16,32,128]{2,1,0:T(8,128)(2,1)}, u32[]{:S(2)}) copy-start(bf16[16,32,128]{2,1,0:T(8,128)(2,1)} %pair_in.1) | copy-start | bytes 393220
  37.0 1.0 %copy-start = (bf16[1024,128]{1,0:T(8,128)(2,1)S(1)}, bf16[1024,128]{1,0:T(8,128)(2,1)}, u32[]{:S(2)}) copy-start(bf16[1024,128]{1,0:T(8,128)(2,1)} %weight.1) | copy-start | bytes 786436
  37.0 1.0 %copy-start.1 = (bf16[128,512]{1,0:T(8,128)(2,1)S(1)}, bf16[128,512]{1,0:T(8,128)(2,1)}, u32[]{:S(2)}) copy-start(bf16[128,512]{1,0:T(8,128)(2,1)} %up.1) | copy-start | bytes 393220
  41.7 8.5 %collective-permute-start = (bf16[64,1024]{1,0:T(8,128)(2,1)S(1)}, bf16[64,1024]{1,0:T(8,128)(2,1)S(1)}, u32[]{:S(2)}, u32[]{:S(2)}) collective-permute-start(bf16[64,1024]{1,0:T(8,128)(2,1)S(1)} %get-tuple-element.22), channel_id=1, source_target_pairs={{0,256},{16,272},{32,288},{48,304},{64,320},{80,336},{96,352},{112... | collective-permute-start | bytes 393224 | tf_op jit(solution)/shard_map/ppermute | solution.py:240
  46.3 10.0 %all-to-all-start.1 = ((bf16[16,8,512]{2,1,0:T(8,128)(2,1)}), bf16[16,8,512]{2,1,0:T(8,128)(2,1)S(1)}, u32[]{:S(2)}, u32[]{:S(2)}) async-start(bf16[16,8,512]{2,1,0:T(8,128)(2,1)} %bitcast.2), calls=%async_computation.1 | async-start | bytes 262144 | tf_op jit(solution)/shard_map/all_to_all | solution.py:184
  56.3 18.8 %all-to-all-start.2 = ((bf16[16,4,1024]{2,1,0:T(4,128)(2,1)}), bf16[16,4,1024]{2,1,0:T(4,128)(2,1)S(1)}, u32[]{:S(2)}, u32[]{:S(2)}) async-start(bf16[16,4,1024]{2,1,0:T(4,128)(2,1)} %shard_map.116), calls=%async_computation.2 | async-start | bytes 262144 | tf_op jit(solution)/shard_map/all_to_all | solution.py:184
